TPU v7x, 32 devices: a whole 2x2x4 slice. The times are simulated.
32 devices in a mesh: req: 16 (over z, x, core), tp: 2 (over y).
Axes of the slice: x: 2, y: 2, z: 4, core: 2. Of those that a mesh axis runs over, the one named last changes fastest.
Arguments:
- decode_tokens: bfloat16 [128, 2048], P('req', 'tp'), may hold values from -6 to 6
- prefill_tokens: bfloat16 [8192, 2048], P('req', 'tp'), may hold values from -6 to 6
- qkv_weight: bfloat16 [2048, 3, 8, 128], P(None, None, 'tp'), may hold values from -0.125 to 0.125
- out_weight: bfloat16 [8, 128, 2048], P('tp'), may hold values from -0.1875 to 0.1875
- prefix_cache: bfloat16 [16, 2048, 8, 2, 128], P('req', None, 'tp'), may hold values from -70 to 70
- page_pool: bfloat16 [256, 128, 8, 2, 128], P('req', None, 'tp'), may hold values from -70 to 70
- page_table: int32 [128, 2], P('req'), may hold values from 0 to 15, as said below
- cached_len: int32 [128], P('req'), may hold values from 1 to 256, as said below
- group_sizes: int32 [16], replicated, may hold values from 1 to 16, 128 in all
- member_order: int32 [128], replicated, may hold values from 0 to 127, each once
- span_start: int32 [16], P('req'), may hold values from 1 to 2048
Outputs:
- decode_out: bfloat16 [128, 2048], P('req', 'tp')
- prefill_out: bfloat16 [8192, 2048], P('req', 'tp')
Inputs may be any that keep to these rules, and one draw needn't show every extreme that they name: `page_table`: the 2 entries of the 8 requests of one index of req name each of that index's 16 pool slots once. `cached_len`: on every index of req one request has exactly 256 private tokens. `group_sizes`: the sizes sum to 128; some group has exactly 16 requests.
All inputs are finite; a program needn't handle non-finite values.
Results may differ from a plain program's by a relative error of at most 0.012.
The roundings to bfloat16 on the way count: a program that leaves them out, or rounds other values in their place, can miss the bound.
Values may be sent and summed in bfloat16 or wider, within the bound.
A program may use at most 128 MiB of HBM per device.

v0:
```python
import jax
import jax.numpy as jnp
from jax import lax
from jax.sharding import PartitionSpec as P

GMAX = 16


def norm_rows(values):
    wide = values.astype(jnp.float32)
    centre = jnp.mean(wide, axis=-1, keepdims=True)
    spread = jnp.mean((wide - centre) ** 2, axis=-1, keepdims=True)
    return ((wide - centre) * lax.rsqrt(spread + 1e-05)).astype(jnp.bfloat16)


def rotary(values, places):
    half_dim = values.shape[-1] // 2
    inverse = 10000.0 ** (-(jnp.arange(half_dim, dtype=jnp.float32) / half_dim))
    angles = places.astype(jnp.float32)[:, None] * inverse[None, :]
    cosine = jnp.cos(angles)[:, None, :]
    sine = jnp.sin(angles)[:, None, :]
    first = values[..., :half_dim]
    second = values[..., half_dim:]
    return jnp.concatenate(
        [first * cosine - second * sine, second * cosine + first * sine], axis=-1
    )


def project(normed, weight):
    flat = weight.reshape(weight.shape[0], -1)
    mixed = jnp.dot(normed, flat, preferred_element_type=jnp.float32)
    return mixed.reshape(normed.shape[0], 3, weight.shape[2], weight.shape[3])


def local(
    decode_tokens,
    prefill_tokens,
    qkv_weight,
    out_weight,
    prefix_cache,
    page_pool,
    page_table,
    cached_len,
    group_sizes,
    member_order,
    span_start,
):
    heads_here = qkv_weight.shape[2]
    head_dim = qkv_weight.shape[3]
    score_scale = head_dim ** (-0.5)
    prefix_len = prefix_cache.shape[1]
    block_rows = prefill_tokens.shape[0]
    dec_count = decode_tokens.shape[0]
    dec_rows, pre_rows = (
        lax.all_gather(decode_tokens, "tp", axis=1, tiled=True),
        lax.all_gather(prefill_tokens, "tp", axis=1, tiled=True),
    )
    dec_qkv = project(norm_rows(dec_rows), qkv_weight)
    pre_qkv = project(norm_rows(pre_rows), qkv_weight)
    dec_places = prefix_len + cached_len
    dec_query = rotary(dec_qkv[:, 0], dec_places).astype(jnp.bfloat16)
    dec_key = rotary(dec_qkv[:, 1], dec_places).astype(jnp.bfloat16)
    dec_value = dec_qkv[:, 2].astype(jnp.bfloat16)
    pre_places = span_start[0] + jnp.arange(block_rows, dtype=jnp.int32)
    pre_query = rotary(pre_qkv[:, 0], pre_places).astype(jnp.bfloat16)
    pre_key = rotary(pre_qkv[:, 1], pre_places).astype(jnp.bfloat16)
    pre_value = pre_qkv[:, 2].astype(jnp.bfloat16)
    prefix_keys = prefix_cache[0, :, :, 0]
    prefix_values = prefix_cache[0, :, :, 1]
    all_queries = lax.all_gather(dec_query, "req", axis=0, tiled=True)
    every_count = all_queries.shape[0]
    member_here = lax.axis_index("req")
    group_ends = jnp.cumsum(group_sizes)
    group_begin = group_ends - group_sizes
    first_rank = group_begin[member_here]
    member_count = group_sizes[member_here]
    padded = jnp.concatenate([member_order, jnp.zeros((GMAX,), jnp.int32)])
    members = lax.dynamic_slice_in_dim(padded, first_rank, GMAX)
    present = jnp.arange(GMAX, dtype=jnp.int32) < member_count
    chosen = all_queries[members]
    far_scores = (
        jnp.einsum("ghd,phd->hgp", chosen, prefix_keys, preferred_element_type=jnp.float32)
        * score_scale
    )
    far_peak = jnp.max(far_scores, axis=-1)
    far_weights = jnp.exp(far_scores - far_peak[..., None])
    far_total = jnp.sum(far_weights, axis=-1)
    far_numer = jnp.einsum(
        "hgp,phd->ghd",
        far_weights.astype(jnp.bfloat16),
        prefix_values,
        preferred_element_type=jnp.float32,
    )
    far_numer = jnp.where(present[:, None, None], far_numer, 0.0)
    far_peak_rows = jnp.where(present[:, None], jnp.transpose(far_peak), 0.0)
    far_total_rows = jnp.where(present[:, None], jnp.transpose(far_total), 0.0)
    spread_numer = jax.ops.segment_sum(far_numer, members, num_segments=every_count)
    spread_peak = jax.ops.segment_sum(far_peak_rows, members, num_segments=every_count)
    spread_total = jax.ops.segment_sum(far_total_rows, members, num_segments=every_count)
    got_numer, got_peak, got_total = (
        lax.psum_scatter(spread_numer, "req", scatter_dimension=0, tiled=True),
        lax.psum_scatter(spread_peak, "req", scatter_dimension=0, tiled=True),
        lax.psum_scatter(spread_total, "req", scatter_dimension=0, tiled=True),
    )
    pages = page_pool[page_table].reshape(dec_count, -1, heads_here, 2, head_dim)
    near_scores = (
        jnp.einsum(
            "rhd,rthd->rht", dec_query, pages[:, :, :, 0], preferred_element_type=jnp.float32
        )
        * score_scale
    )
    valid = jnp.arange(pages.shape[1], dtype=jnp.int32)[None, :] < cached_len[:, None]
    near_scores = jnp.where(valid[:, None, :], near_scores, -1e30)
    own_score = (
        jnp.sum(dec_query.astype(jnp.float32) * dec_key.astype(jnp.float32), axis=-1) * score_scale
    )
    near_peak = jnp.maximum(jnp.max(near_scores, axis=-1), own_score)
    near_weights = jnp.where(valid[:, None, :], jnp.exp(near_scores - near_peak[..., None]), 0.0)
    own_weight = jnp.exp(own_score - near_peak)
    near_total = jnp.sum(near_weights, axis=-1) + own_weight
    near_numer = jnp.einsum(
        "rht,rthd->rhd",
        near_weights.astype(jnp.bfloat16),
        pages[:, :, :, 1],
        preferred_element_type=jnp.float32,
    )
    near_numer = near_numer + own_weight.astype(jnp.bfloat16).astype(jnp.float32)[
        ..., None
    ] * dec_value.astype(jnp.float32)
    top = jnp.maximum(got_peak, near_peak)
    far_factor = jnp.exp(got_peak - top)
    near_factor = jnp.exp(near_peak - top)
    dec_context = (
        (far_factor[..., None] * got_numer + near_factor[..., None] * near_numer)
        / (far_factor * got_total + near_factor * near_total)[..., None]
    ).astype(jnp.bfloat16)
    keys_all = jnp.concatenate([prefix_keys, pre_key], axis=0)
    values_all = jnp.concatenate([prefix_values, pre_value], axis=0)
    block_scores = (
        jnp.einsum("qhd,khd->hqk", pre_query, keys_all, preferred_element_type=jnp.float32)
        * score_scale
    )
    key_places = jnp.arange(prefix_len + block_rows, dtype=jnp.int32)
    row_places = jnp.arange(block_rows, dtype=jnp.int32)
    allowed = jnp.where(
        key_places[None, :] < prefix_len,
        key_places[None, :] < span_start[0],
        key_places[None, :] - prefix_len <= row_places[:, None],
    )
    block_scores = jnp.where(allowed[None], block_scores, -1e30)
    block_peak = jnp.max(block_scores, axis=-1)
    block_weights = jnp.where(allowed[None], jnp.exp(block_scores - block_peak[..., None]), 0.0)
    block_total = jnp.sum(block_weights, axis=-1)
    block_numer = jnp.einsum(
        "hqk,khd->qhd",
        block_weights.astype(jnp.bfloat16),
        values_all,
        preferred_element_type=jnp.float32,
    )
    pre_context = (block_numer / jnp.transpose(block_total)[:, :, None]).astype(jnp.bfloat16)
    dec_flat = dec_context.reshape(dec_count, heads_here * head_dim)
    pre_flat = pre_context.reshape(block_rows, heads_here * head_dim)
    flat_out = out_weight.reshape(heads_here * head_dim, out_weight.shape[2])
    dec_terms = jnp.dot(dec_flat, flat_out, preferred_element_type=jnp.float32)
    pre_terms = jnp.dot(pre_flat, flat_out, preferred_element_type=jnp.float32)
    dec_summed, pre_summed = (
        lax.psum_scatter(dec_terms, "tp", scatter_dimension=1, tiled=True),
        lax.psum_scatter(pre_terms, "tp", scatter_dimension=1, tiled=True),
    )
    decode_out = dec_summed.astype(jnp.bfloat16)
    prefill_out = pre_summed.astype(jnp.bfloat16)
    return (decode_out, prefill_out)


def solution(mesh):
    placed = (
        P("req", "tp"),
        P("req", "tp"),
        P(None, None, "tp", None),
        P("tp", None, None),
        P("req", None, "tp", None, None),
        P("req", None, "tp", None, None),
        P("req", None),
        P("req"),
        P(),
        P(),
        P("req"),
    )
    return jax.shard_map(
        local,
        mesh=mesh,
        in_specs=placed,
        out_specs=(P("req", "tp"), P("req", "tp")),
        check_vma=False,
    )
```

profile of v0, /device:TPU:0, one launch (start us, length us, event | category | flops | bytes accessed | tf_op | source)
XLA Modules:
  0.0 311.1 jit_solution(9846136058343063142)
XLA Ops:
  8.1 1.4 dynamic_slice.11
  9.5 0.6 iota_compare_fusion.4
  10.1 0.7 add_convert_fusion.5
  10.8 0.7 copy.105
  11.5 0.1 reduce
  11.7 0.7 sub.79
  12.3 0.6 dynamic_slice.9
  14.8 0.7 compare_select_fusion.1
  15.6 5.6 %all_gather.9 = bf16[8,2048]{1,0:T(8,128)(2,1)S(1)} all-gather(bf16[8,1024]{1,0:T(8,128)(2,1)} %param.11), channel_id=1, replica_groups=mesh['req'=16,'tp'=2] {'tp'}, dimensions={1}, use_global_device_ids=true | all-gather | bytes 49152 | tf_op jit(solution)/shard_map/all_gather | solution.py:55
  21.2 0.1 convert_reduce_fusion.1
  21.3 0.2 fusion.59
  21.5 11.0 %reshape.286 = bf16[2048,1536]{1,0:T(8,128)(2,1)} reshape(bf16[2048,3,4,128]{3,2,1,0:T(4,128)(2,1)} %param.13) | data formatting | bytes 12582912 | tf_op jit(solution)/shard_map/reshape | solution.py:30
  32.6 8.7 %copy.106 = bf16[1536,2048]{1,0:T(8,128)(2,1)} copy(bf16[1536,2048]{0,1:T(8,128)(2,1)} %bitcast.96) | data formatting | bytes 12582912 | tf_op jit(solution)/shard_map/dot_general | solution.py:31
  41.2 4.6 %fusion.62 = f32[8,3,4,128]{3,0,2,1:T(8,128)S(1)} fusion(bf16[3,4,128,2048]{3,2,1,0:T(8,128)(2,1)} %bitcast.94, bf16[8,2048]{1,0:T(8,128)(2,1)S(1)} %all_gather.9, f32[8]{0:T(128)S(1)} %add_rsqrt_fusion.1, f32[8]{0:T(128)S(1)} %broadcast_multiply_fusion.1), kind=kOutput, calls=%fused_computation.74 | convolution fusion | flops 50397184 | bytes 6373440 | tf_op jit(solution)/shard_map/dot_general | solution.py:31
  45.9 0.1 multiply_cosine_fusion.1
  46.0 0.1 subtract_convert_fusion.3
  46.1 0.2 multiply_reduce_fusion
  46.3 22.4 %all_gather.10 = bf16[128,4,128]{2,0,1:T(8,128)(2,1)S(1)} all-gather(bf16[8,4,128]{2,0,1:T(8,128)(2,1)S(1)} %get-tuple-element.12), channel_id=1, replica_groups=mesh['req'=16,'tp'=2] {'req'}, dimensions={0}, use_global_device_ids=true | all-gather | bytes 139264 | tf_op jit(solution)/shard_map/all_gather | solution.py:70
  68.7 0.1 copy.107
  68.8 6.8 %fusion.99 = (bf16[1,2048,4,1,128]{4,3,2,1,0:T(2,128)(2,1)S(1)}, bf16[1,2048,4,1,128]{4,3,2,1,0:T(2,128)(2,1)}) fusion(bf16[1,2048,4,2,128]{4,3,2,1,0:T(2,128)(2,1)S(1)} %copy-done.2), kind=kLoop, calls=%fused_computation.146 | loop fusion | bytes 8388608 | tf_op jit(solution)/shard_map/slice | solution.py:68
  75.6 1.7 copy.174
  77.3 0.6 gather_fusion
  77.9 2.3 fusion.102
  80.2 2.9 fusion.39
  83.1 1.1 scatter_fusion
  84.2 0.7 copy.118
  85.0 0.5 all-gather.2.cloned.1.call-update
  85.6 0.1 iota_compare_fusion.3
  85.7 0.2 fusion.53
  85.9 10.7 %copy.137 = bf16[1,2048,4,1,128]{1,4,2,0,3:T(8,128)(2,1)} copy(bf16[1,2048,4,1,128]{4,3,2,1,0:T(2,128)(2,1)} %get-tuple-element.14) | data formatting | bytes 4194304 | tf_op jit(solution)/shard_map/squeeze | solution.py:69
  97.3 0.1 copy.111
  97.4 0.1 reshape.299
  97.5 12.2 %gather_fusion.1 = bf16[16,128,4,2,128]{4,3,2,1,0:T(2,128)(2,1)} fusion(bf16[16,128,4,2,128]{4,3,2,1,0:T(2,128)(2,1)} %param.16, s32[1024]{0:T(1024)S(1)} %pad_clamp_fusion), kind=kCustom, calls=%fused_computation.1 | custom fusion | bytes 8388672 | tf_op jit(solution)/shard_map/gather | solution.py:105
  109.6 3.3 %copy.112 = bf16[16,128,4,2,128]{4,1,0,3,2:T(8,128)(2,1)S(1)} copy(bf16[16,128,4,2,128]{4,3,2,1,0:T(2,128)(2,1)} %gather_fusion.1) | data formatting | bytes 8388608 | tf_op jit(solution)/shard_map/gather | solution.py:105
  112.9 2.3 fusion.100
  115.2 0.1 copy.120
  115.3 0.1 copy.110
  115.4 0.7 scatter_custom_fusion
  116.0 0.7 scatter_custom_fusion.2
  116.7 0.6 dynamic-slice
  118.0 58.9 %all-reduce.3 = (f32[128,4]{1,0:T(8,128)S(1)}, f32[128,4]{1,0:T(8,128)S(1)}) all-reduce(f32[128,4]{1,0:T(8,128)S(1)} %scatter_custom_fusion, f32[128,4]{1,0:T(8,128)S(1)} %scatter_custom_fusion.2), channel_id=2, replica_groups=mesh['req'=16,'tp'=2] {'req'}, use_global_device_ids=true, to_apply=%region_5.6.clone | all-reduce | flops 1024 | bytes 8192
  176.9 0.1 copy.121
  177.0 0.1 copy.115
  177.1 2.2 fusion.27
  179.3 0.1 fusion.74
  179.4 0.2 fusion.72
  179.6 1.8 multiply_cosine_fusion
  181.3 2.0 fusion.25
  183.3 2.0 fusion.7
  185.3 1.8 convolution_bitcast_fusion.1
  187.2 2.1 convert_reduce_fusion
  189.3 2.3 fusion.10
  191.6 5.9 %fusion.22 = f32[512,3,4,128]{0,3,2,1:T(8,128)S(1)} fusion(bf16[3,4,128,2048]{3,2,1,0:T(8,128)(2,1)} %bitcast.95, bf16[512,2048]{1,0:T(8,128)(2,1)S(1)} %copy-done.3, f32[512]{0:T(512)S(1)} %add_rsqrt_fusion, f32[512]{0:T(512)S(1)} %broadcast_multiply_fusion), kind=kOutput, calls=%fused_computation.35 | convolution fusion | flops 3225419776 | bytes 11538432 | tf_op jit(solution)/shard_map/dot_general | solution.py:31
  197.5 0.9 fusion.48
  198.4 1.7 fusion.101
  200.0 1.5 copy.135
  201.6 2.5 copy.136
  204.1 2.5 subtract_convert_fusion.1
  206.7 8.6 %fusion.15 = f32[4,512,2560]{2,1,0:T(8,128)} fusion(bf16[512,4,64]{2,0,1:T(8,128)(2,1)S(1)} %get-tuple-element.23, bf16[512,4,64]{2,0,1:T(8,128)(2,1)S(1)} %get-tuple-element.24, bf16[2048,4,128]{2,0,1:T(8,128)(2,1)S(1)} %bitcast.98, bf16[512,4,64]{2,0,1:T(8,128)(2,1)S(1)} %get-tuple-element.20, bf16[512,4,64]{2,0,1:T(8,128)(2,1)S(1)} %get-tuple-element.19), kind=kOutput, calls=%fused_computation.26 | convolution fusion | flops 1351090176 | bytes 24117248 | tf_op jit(solution)/shard_map/qhd,khd->hqk/dot_general | solution.py:140
  215.3 22.7 %fusion.103 = (f32[4,512]{1,0:T(4,128)S(1)}, bf16[4,512,2560]{2,1,0:T(8,128)(2,1)}) fusion(f32[4,512,2560]{2,1,0:T(8,128)} %fusion.15, pred[512,2560]{1,0:T(8,128)(4,1)S(1)} %copy-done.4), kind=kOutput, calls=%fused_computation.150 | output fusion | flops 41945600 | bytes 32776192 | tf_op jit(solution)/shard_map/sub | solution.py:152
  238.0 11.1 %convolution_bitcast_fusion = f32[512,2048]{1,0:T(8,128)} fusion(bf16[4,128,2048]{2,1,0:T(8,128)(2,1)S(1)} %copy-done, bf16[4,512,2560]{2,1,0:T(8,128)(2,1)} %get-tuple-element.44, bf16[512,4,128]{0,2,1:T(8,128)(2,1)S(1)} %copy-done.5, bf16[2048,4,128]{0,2,1:T(8,128)(2,1)} %bitcast.102, f32[512,4]{0,1:T(4,128)S(1)} %bitcast.105), kind=kOutput, calls=%fused_computation.22 | convolution fusion | flops 2421686272 | bytes 19406848 | tf_op jit(solution)/shard_map/dot_general | solution.py:165
  249.2 1.4 convert_element_type.93
  250.6 50.2 %reduce-scatter.8.cloned.1.call-done = f32[512,1024]{1,0:T(8,128)} async-done(((f32[512,2048]{1,0:T(8,128)}), f32[512,1024]{1,0:T(8,128)}) %reduce-scatter.8.cloned.1.call-update) | async-done | bytes 2097168 | tf_op jit(solution)/shard_map/reduce_scatter | solution.py:168
  300.8 2.7 convert_element_type.100
  (47 shorter events, 0.5 us)
Async XLA Ops:
  8.0 177.3 %copy-start = (bf16[4,128,2048]{2,1,0:T(8,128)(2,1)S(1)}, bf16[4,128,2048]{2,1,0:T(8,128)(2,1)}, u32[]{:S(2)}) copy-start(bf16[4,128,2048]{2,1,0:T(8,128)(2,1)} %param.14) | copy-start | bytes 6291460
  8.0 177.3 %reduce-scatter.4.cloned.1.call-start = ((), (), s32[]{:S(2)}) async-start(), calls=%async_computation.3 | async-start | bytes 278528 | tf_op jit(solution)/shard_map/reduce_scatter | solution.py:101
  41.2 27.6 %copy-start.2 = (bf16[1,2048,4,2,128]{4,3,2,1,0:T(2,128)(2,1)S(1)}, bf16[1,2048,4,2,128]{4,3,2,1,0:T(2,128)(2,1)}, u32[]{:S(2)}) copy-start(bf16[1,2048,4,2,128]{4,3,2,1,0:T(2,128)(2,1)} %param.15) | copy-start | bytes 12582916
  77.3 8.3 %copy-start.7 = (s32[8]{0:T(128)S(1)}, s32[8]{0:T(128)}, u32[]{:S(2)}) copy-start(s32[8]{0:T(128)} %param.18) | copy-start | bytes 100
  85.0 12.3 %copy-start.6 = (s32[8,2]{0,1:T(2,128)S(1)}, s32[8,2]{0,1:T(2,128)}, u32[]{:S(2)}) copy-start(s32[8,2]{0,1:T(2,128)} %param.17) | copy-start | bytes 196
  85.0 102.2 %all-gather.2.cloned.1.call-start = ((), (), s32[]{:S(2)}) async-start(), calls=%async_computation.5 | async-start | bytes 3145728 | tf_op jit(solution)/shard_map/all_gather | solution.py:56
  85.6 163.6 %reduce-scatter.6.cloned.1.call-start = ((), (), s32[]{:S(2)}) async-start(), calls=%async_computation.4 | async-start | bytes 98304 | tf_op jit(solution)/shard_map/reduce_scatter | solution.py:167
  112.9 3.8 %copy-start.8 = (u32[32]{0:T(128)S(1)}, u32[32]{0:T(128)}, u32[]{:S(2)}) copy-start(u32[32]{0:T(128)} %constant.62) | copy-start | bytes 388
  187.1 113.7 %reduce-scatter.8.cloned.1.call-start = ((), (), s32[]{:S(2)}) async-start(), calls=%async_computation.6 | async-start | bytes 6291456 | tf_op jit(solution)/shard_map/reduce_scatter | solution.py:168
  187.2 4.4 %copy-start.3 = (bf16[512,2048]{1,0:T(8,128)(2,1)S(1)}, bf16[512,2048]{1,0:T(8,128)(2,1)}, u32[]{:S(2)}) copy-start(bf16[512,2048]{1,0:T(8,128)(2,1)} %all-gather.2.cloned.1.call-done) | copy-start | bytes 6291460
  204.1 2.5 copy-start.1
  206.7 8.6 %copy-start.4 = (pred[512,2560]{1,0:T(8,128)(4,1)S(1)}, pred[512,2560]{1,0:T(8,128)(4,1)}, u32[]{:S(2)}) copy-start(pred[512,2560]{1,0:T(8,128)(4,1)} %fusion.7) | copy-start | bytes 3932164
  215.3 22.7 %copy-start.5 = (bf16[512,4,128]{0,2,1:T(8,128)(2,1)S(1)}, bf16[512,4,128]{0,2,1:T(8,128)(2,1)}, u32[]{:S(2)}) copy-start(bf16[512,4,128]{0,2,1:T(8,128)(2,1)} %fusion.48) | copy-start | bytes 1572868
Sparse Core Ops, SparseCore 0:
  85.1 52.6 reduce-scatter.3
Sparse Core Ops, SparseCore 1:
  87.0 30.2 all-gather.1
  187.2 7.1 reduce-scatter.5
  249.3 51.4 reduce-scatter.7
where the time goes:
time: 312 us; the launch traced here: 311 us
  blocking collectives  86.9 us (28%)
  local copies, waits for them, and re-layouts  68.5 us (22%)
  waiting for transfers between devices  50.8 us (16%)
  other arithmetic  44.1 us (14%)
  matrix products  41.4 us (13%)
  between operations  19.2 us (6%)
    unnamed x1, blocking collectives  58.9 us
    reduce_scatter x1, waiting for transfers between devices, local(): lax.psum_scatter(pre_terms, 'tp', scatter_dimension=1, tiled=True)  50.2 us
    sub x1, other arithmetic, local(): block_scores - block_peak[..., None]  22.7 us
    all_gather x1, blocking collectives, local(): all_queries = lax.all_gather(dec_query, 'req', axis=0, tiled=True)  22.4 us
    gather x2, local copies, waits for them, and re-layouts, local(): page_pool[page_table].reshape(dec_count, -1, heads_here, 2, head_dim)  15.4 us
    dot_general x1, matrix products, local(): pre_terms = jnp.dot(pre_flat, flat_out, preferred_element_type=jnp.float32)  11.1 us
    reshape x1, local copies, waits for them, and re-layouts, project(): flat = weight.reshape(weight.shape[0], -1)  11 us
    squeeze x1, local copies, waits for them, and re-layouts, local(): prefix_values = prefix_cache[0, :, :, 1]  10.7 us
  transfers between devices with their start and end apart: 4, of which 1 were waited for; matrix products, arithmetic and copies ran while one was open for 34% of the time, Pallas kernels for 0%

commit v1 on v0

v1 whole, which is shorter than its diff:
```python
import functools
import math

import jax
import jax.numpy as jnp
from jax import lax
from jax.experimental import pallas as pl
from jax.experimental.pallas import tpu as pltpu
from jax.sharding import PartitionSpec as P

GMAX = 16
F32, BF16 = jnp.float32, jnp.bfloat16
MESH = pl.DeviceIdType.MESH
VM = pl.BlockSpec(memory_space=pltpu.VMEM)
SM = pl.BlockSpec(memory_space=pltpu.SMEM)
BIG = 56 << 20


def dot(a, b):
    return jnp.dot(a, b, preferred_element_type=F32)


def dot_t(a, b):
    return lax.dot_general(a, b, (((1,), (1,)), ((), ())), preferred_element_type=F32)


def spread_rows(src, dst, tokens, group):
    piece = 16
    while piece * 2 * group <= 256 and piece * 2 <= tokens:
        piece *= 2
    rows = piece * group
    at = lax.broadcasted_iota(jnp.int32, (rows, rows), 0)
    col = lax.broadcasted_iota(jnp.int32, (rows, rows), 1)
    shift = piece.bit_length() - 1
    want = (at & (piece - 1)) * group + lax.shift_right_logical(at, shift)
    pick = jnp.where(col == want, 1.0, 0.0).astype(BF16)
    for k in range(tokens // piece):
        moved = dot(pick, src[k * rows : (k + 1) * rows, :]).astype(BF16)
        for g in range(group):
            dst[k * piece : (k + 1) * piece, g * 128 : (g + 1) * 128] = moved[
                g * piece : (g + 1) * piece, :
            ]


def prep_kernel(groups, tokens, *refs):
    half = len(refs) // 2
    for src, dst, g in zip(refs[:half], refs[half:], groups):
        spread_rows(src, dst, tokens, g)


def prep(arrays, groups, total):
    steps = 16
    tokens = total // steps
    return pl.pallas_call(
        functools.partial(prep_kernel, groups, tokens),
        grid=(steps,),
        out_shape=[jax.ShapeDtypeStruct((total, g * 128), BF16) for g in groups],
        in_specs=[pl.BlockSpec((tokens * g, 128), lambda i: (i, 0)) for g in groups],
        out_specs=[pl.BlockSpec((tokens, g * 128), lambda i: (i, 0)) for g in groups],
        compiler_params=pltpu.CompilerParams(vmem_limit_bytes=BIG),
        cost_estimate=pl.CostEstimate(
            flops=int(2e9), bytes_accessed=int(4 * total * 128 * sum(groups)), transcendentals=0
        ),
        name="prep",
    )(*arrays)


def gather_kernel(axis, count, x_ref, out_ref, send, recv):
    me = lax.axis_index(axis)
    barrier = pltpu.get_barrier_semaphore()

    def greet(k, _):
        pl.semaphore_signal(
            barrier, inc=1, device_id={axis: lax.rem(me + k, count)}, device_id_type=MESH
        )
        return 0

    lax.fori_loop(1, count, greet, 0)
    pl.semaphore_wait(barrier, count - 1)

    def make(k):
        return pltpu.make_async_remote_copy(
            src_ref=x_ref,
            dst_ref=out_ref.at[me],
            send_sem=send.at[k],
            recv_sem=recv.at[k],
            device_id={axis: lax.rem(me + k, count)},
            device_id_type=MESH,
        )

    def go(k, _):
        make(k).start()
        return 0

    lax.fori_loop(1, count, go, 0)
    out_ref[me] = x_ref[...]

    def done(k, _):
        make(k).wait()
        return 0

    lax.fori_loop(1, count, done, 0)


def gather_all(x, axis, count, ident):
    return pl.pallas_call(
        functools.partial(gather_kernel, axis, count),
        out_shape=jax.ShapeDtypeStruct((count,) + x.shape, x.dtype),
        in_specs=[VM],
        out_specs=VM,
        scratch_shapes=[pltpu.SemaphoreType.DMA((count,)), pltpu.SemaphoreType.DMA((count,))],
        compiler_params=pltpu.CompilerParams(collective_id=ident, has_side_effects=True),
        name="gather_all",
    )(x)


def normed_parts(parts):
    wide = [p.astype(F32) for p in parts]
    width = sum(p.shape[1] for p in parts)
    centre = sum(jnp.sum(w, axis=1, keepdims=True) for w in wide) * (1.0 / width)
    moved = [w - centre for w in wide]
    spread = sum(jnp.sum(m * m, axis=1, keepdims=True) for m in moved) * (1.0 / width)
    gain = lax.rsqrt(spread + 1e-05)
    return [(m * gain).astype(BF16) for m in moved]


def qkv_rows(parts, offs, w_ref):
    out = None
    for k, part in enumerate(normed_parts(parts)):
        depth = part.shape[1]
        rows = w_ref[pl.ds(pl.multiple_of(offs[k], 128), depth), :]
        term = dot(part, rows)
        out = term if out is None else out + term
    return out


def turn(y, cos, sin):
    return y * cos + pltpu.roll(y, 64, 1) * sin


def dec_qkv_kernel(n, heads, offs, *refs):
    parts = [r[...] for r in refs[:n]]
    w_ref, cos, sin, q_out, k_out, v_out = refs[n:]
    y = qkv_rows(parts, [offs[k] for k in range(n)], w_ref)
    c, s = cos[...], sin[...]
    for h in range(heads):
        here = slice(h * 128, (h + 1) * 128)
        q_out[:, here] = turn(y[:, h * 128 : (h + 1) * 128], c, s).astype(BF16)
        k_out[:, here] = turn(
            y[:, (heads + h) * 128 : (heads + h + 1) * 128], c, s
        ).astype(BF16)
        v_out[:, here] = y[:, (2 * heads + h) * 128 : (2 * heads + h + 1) * 128].astype(BF16)


def dec_attn_kernel(heads, scale, allq, members, prefix, q, knew, vnew, pool, table, lens, far, near):
    every = allq.shape[0]
    sel = jnp.where(
        members[...] == lax.broadcasted_iota(jnp.int32, (GMAX, every), 1), 1.0, 0.0
    ).astype(BF16)
    chosen = dot(sel, allq[...]).astype(BF16)
    rows = q.shape[0]
    slots = pool.shape[0]
    t = lax.broadcasted_iota(jnp.int32, (rows, slots), 1)
    page, off = lax.shift_right_logical(t, 7), t & 127
    valid = None
    for j in range(table.shape[1]):
        one = (page == table[:, j : j + 1]) & (off + j * 128 < lens[...])
        valid = one if valid is None else valid | one
    lane_f = lax.broadcasted_iota(jnp.int32, (GMAX, 128), 1)
    lane_n = lax.broadcasted_iota(jnp.int32, (rows, 128), 1)
    far_stat = jnp.zeros((GMAX, 128), F32)
    near_stat = jnp.zeros((rows, 128), F32)
    for h in range(heads):
        here = slice(h * 128, (h + 1) * 128)
        kcol = slice(h * 256, h * 256 + 128)
        vcol = slice(h * 256 + 128, h * 256 + 256)
        s = dot_t(chosen[:, here], prefix[:, kcol]) * scale
        m = jnp.max(s, axis=1, keepdims=True)
        w = jnp.exp(s - m)
        far_stat = jnp.where(lane_f == h, m, far_stat)
        far_stat = jnp.where(
            lane_f == heads + h, jnp.sum(w, axis=1, keepdims=True), far_stat
        )
        far[:, here] = dot(w.astype(BF16), prefix[:, vcol])
        qh = q[:, here]
        s = jnp.where(valid, dot_t(qh, pool[:, kcol]) * scale, -1e30)
        own = (
            jnp.sum(qh.astype(F32) * knew[:, here].astype(F32), axis=1, keepdims=True) * scale
        )
        m = jnp.maximum(jnp.max(s, axis=1, keepdims=True), own)
        w = jnp.where(valid, jnp.exp(s - m), 0.0)
        ow = jnp.exp(own - m)
        near_stat = jnp.where(lane_n == h, m, near_stat)
        near_stat = jnp.where(
            lane_n == heads + h, jnp.sum(w, axis=1, keepdims=True) + ow, near_stat
        )
        near[:, here] = dot(w.astype(BF16), pool[:, vcol]) + ow.astype(BF16).astype(
            F32
        ) * vnew[:, here].astype(F32)
    far[:, heads * 128 :] = far_stat
    near[:, heads * 128 :] = near_stat


def merge_kernel(heads, base, got, owners, near, ctx):
    rows = near.shape[0]
    slots = got.shape[0]
    want = base[0] + lax.broadcasted_iota(jnp.int32, (rows, slots), 0)
    pick = jnp.where(owners[...] == want, 1.0, 0.0)
    far = jnp.dot(
        pick, got[...], preferred_element_type=F32, precision=lax.Precision.HIGHEST
    )
    fs, ns = far[:, heads * 128 :], near[:, heads * 128 :]
    for h in range(heads):
        here = slice(h * 128, (h + 1) * 128)
        mp, lp = fs[:, h : h + 1], fs[:, heads + h : heads + h + 1]
        ml, ll = ns[:, h : h + 1], ns[:, heads + h : heads + h + 1]
        top = jnp.maximum(mp, ml)
        a, b = jnp.exp(mp - top), jnp.exp(ml - top)
        ctx[:, here] = (
            (a * far[:, here] + b * near[:, here]) / (a * lp + b * ll)
        ).astype(BF16)


def prefill_kernel(n, heads, rows, scale, scal, *refs):
    parts = [r[...] for r in refs[:n]]
    w_ref, cos, sin, prefix, ctx, kself, vself = refs[n:]
    step = pl.program_id(0)
    start = scal[n]

    @pl.when(step == 0)
    def _():
        kself[...] = jnp.zeros_like(kself)
        vself[...] = jnp.zeros_like(vself)

    y = qkv_rows(parts, [scal[k] for k in range(n)], w_ref)
    c, s = cos[...], sin[...]
    at = pl.ds(pl.multiple_of(step * rows, rows), rows)
    total = kself.shape[0]
    far_len = prefix.shape[0]
    far_bias = jnp.where(
        lax.broadcasted_iota(jnp.int32, (1, far_len), 1) < start, 0.0, -1e30
    )
    near_ok = lax.broadcasted_iota(jnp.int32, (rows, total), 1) <= (
        step * rows + lax.broadcasted_iota(jnp.int32, (rows, total), 0)
    )
    factor = scale * math.log2(math.e)
    for h in range(heads):
        here = slice(h * 128, (h + 1) * 128)
        kcol = slice(h * 256, h * 256 + 128)
        vcol = slice(h * 256 + 128, h * 256 + 256)
        qh = turn(y[:, h * 128 : (h + 1) * 128], c, s).astype(BF16)
        kself[at, here] = turn(
            y[:, (heads + h) * 128 : (heads + h + 1) * 128], c, s
        ).astype(BF16)
        vself[at, here] = y[:, (2 * heads + h) * 128 : (2 * heads + h + 1) * 128].astype(BF16)
        sf = dot_t(qh, prefix[:, kcol]) + far_bias
        sn = jnp.where(near_ok, dot_t(qh, kself[:, here]), -1e30)
        m = jnp.maximum(
            jnp.max(sf, axis=1, keepdims=True), jnp.max(sn, axis=1, keepdims=True)
        )
        wf = jnp.exp2((sf - m) * factor)
        wn = jnp.exp2((sn - m) * factor)
        l = jnp.sum(wf, axis=1, keepdims=True) + jnp.sum(wn, axis=1, keepdims=True)
        o = dot(wf.astype(BF16), prefix[:, vcol]) + dot(wn.astype(BF16), vself[:, here])
        ctx[:, here] = (o / l).astype(BF16)


def out_kernel(n, *refs):
    ctxs, decs, ws = refs[:n], refs[n : 2 * n], refs[2 * n : 3 * n]
    pre_out, dec_out = refs[3 * n :]
    pre_out[...] = sum(dot(c[...], w[...]) for c, w in zip(ctxs, ws)).astype(pre_out.dtype)

    @pl.when(pl.program_id(0) == 0)
    def _():
        dec_out[...] = sum(dot(c[...], w[...]) for c, w in zip(decs, ws)).astype(dec_out.dtype)


def tables(places):
    inverse = 10000.0 ** (-(jnp.arange(64, dtype=F32) / 64))
    angles = places.astype(F32)[:, None] * inverse[None, :]
    c, s = jnp.cos(angles), jnp.sin(angles)
    return jnp.concatenate([c, c], axis=1), jnp.concatenate([-s, s], axis=1)


def local(
    n_req,
    n_tp,
    decode_tokens,
    prefill_tokens,
    qkv_weight,
    out_weight,
    prefix_cache,
    page_pool,
    page_table,
    cached_len,
    group_sizes,
    member_order,
    span_start,
):
    heads = qkv_weight.shape[2]
    width = heads * 128
    features = qkv_weight.shape[0]
    scale = 128 ** (-0.5)
    prefix_len = prefix_cache.shape[1]
    block_rows, share = prefill_tokens.shape
    dec_count = decode_tokens.shape[0]
    me = lax.axis_index("req")
    side = lax.axis_index("tp")
    swap = [(0, 1), (1, 0)]
    if n_tp == 2:
        dec_parts = [decode_tokens, lax.ppermute(decode_tokens, "tp", swap)]
        pre_parts = [prefill_tokens, lax.ppermute(prefill_tokens, "tp", swap)]
        offs = [side * share, (1 - side) * share]
    else:
        dec_parts = [lax.all_gather(decode_tokens, "tp", axis=1, tiled=True)]
        pre_parts = [lax.all_gather(prefill_tokens, "tp", axis=1, tiled=True)]
        offs = [jnp.int32(0)]
    n = len(offs)
    slots = page_pool.shape[0] * page_pool.shape[1]
    weight, prefix, pool = prep(
        [
            qkv_weight.reshape(-1, 128),
            prefix_cache.reshape(-1, 128),
            page_pool.reshape(-1, 128),
        ],
        [3 * heads, 2 * heads, 2 * heads],
        features,
    ) if features == prefix_len == slots else (
        prep([qkv_weight.reshape(-1, 128)], [3 * heads], features)
        + prep([prefix_cache.reshape(-1, 128)], [2 * heads], prefix_len)
        + prep([page_pool.reshape(-1, 128)], [2 * heads], slots)
    )
    begin = jnp.cumsum(group_sizes) - group_sizes
    slot_at = jnp.arange(GMAX, dtype=jnp.int32)[None, :]
    padded = jnp.concatenate([member_order, jnp.zeros((GMAX,), jnp.int32)])
    owners = jnp.where(
        slot_at < group_sizes[:, None], padded[begin[:, None] + slot_at], -1
    )
    members = lax.dynamic_slice_in_dim(owners, me, 1, axis=0).reshape(GMAX, 1)
    dcos, dsin = tables(prefix_len + cached_len)
    pcos, psin = tables(span_start[0] + jnp.arange(block_rows, dtype=jnp.int32))
    off_arr = jnp.stack(offs).astype(jnp.int32)
    row = jax.ShapeDtypeStruct((dec_count, width), BF16)
    dq, dk, dv = pl.pallas_call(
        functools.partial(dec_qkv_kernel, n, heads),
        out_shape=[row, row, row],
        in_specs=[SM] + [VM] * (n + 3),
        out_specs=[VM] * 3,
        compiler_params=pltpu.CompilerParams(vmem_limit_bytes=BIG),
        name="dec_qkv",
    )(off_arr, *dec_parts, weight, dcos, dsin)
    allq = gather_all(dq, "req", n_req, 1).reshape(n_req * dec_count, width)
    far, near = pl.pallas_call(
        functools.partial(dec_attn_kernel, heads, scale),
        out_shape=[
            jax.ShapeDtypeStruct((GMAX, width + 128), F32),
            jax.ShapeDtypeStruct((dec_count, width + 128), F32),
        ],
        in_specs=[VM] * 9,
        out_specs=[VM] * 2,
        compiler_params=pltpu.CompilerParams(vmem_limit_bytes=BIG),
        name="dec_attn",
    )(allq, members, prefix, dq, dk, dv, pool, page_table, cached_len[:, None])
    got = gather_all(far, "req", n_req, 2).reshape(n_req * GMAX, width + 128)
    dec_ctx = pl.pallas_call(
        functools.partial(merge_kernel, heads),
        out_shape=row,
        in_specs=[SM] + [VM] * 3,
        out_specs=VM,
        compiler_params=pltpu.CompilerParams(vmem_limit_bytes=BIG),
        name="merge",
    )((me * dec_count)[None].astype(jnp.int32), got, owners.reshape(1, -1), near)
    flat_out = out_weight.reshape(width, out_weight.shape[2])
    if n_tp == 2:
        theirs = lax.dynamic_slice_in_dim(flat_out, (1 - side) * share, share, axis=1)
        theirs, pre_parts[1] = lax.optimization_barrier((theirs, pre_parts[1]))
        peer_w = lax.ppermute(theirs, "tp", swap)
        own_w = lax.dynamic_slice_in_dim(flat_out, side * share, share, axis=1)
    chunk = min(128, block_rows)
    scal = jnp.concatenate([off_arr, span_start]).astype(jnp.int32)
    whole = lambda a: pl.BlockSpec(a.shape, lambda i: (0, 0), pipeline_mode=pl.Buffered(1))
    band = lambda w: pl.BlockSpec((chunk, w), lambda i: (i, 0))
    pre_ctx = pl.pallas_call(
        functools.partial(prefill_kernel, n, heads, chunk, scale),
        grid=(block_rows // chunk,),
        out_shape=jax.ShapeDtypeStruct((block_rows, width), BF16),
        in_specs=[SM]
        + [band(p.shape[1]) for p in pre_parts]
        + [whole(weight), band(128), band(128), whole(prefix)],
        out_specs=band(width),
        scratch_shapes=[pltpu.VMEM((block_rows, width), BF16)] * 2,
        compiler_params=pltpu.CompilerParams(vmem_limit_bytes=BIG),
        cost_estimate=pl.CostEstimate(
            flops=int(8e9), bytes_accessed=int(13e6), transcendentals=int(5e6)
        ),
        name="prefill",
    )(scal, *pre_parts, weight, pcos, psin, prefix)
    if n_tp == 2:
        pre_ctxs = [pre_ctx, lax.ppermute(pre_ctx, "tp", swap)]
        dec_ctxs = [dec_ctx, lax.ppermute(dec_ctx, "tp", swap)]
        outs_w, kind = [own_w, peer_w], BF16
    else:
        pre_ctxs, dec_ctxs, outs_w, kind = [pre_ctx], [dec_ctx], [flat_out], F32
    m = len(outs_w)
    span = outs_w[0].shape[1]
    pre_out, dec_out = pl.pallas_call(
        functools.partial(out_kernel, m),
        grid=(block_rows // chunk,),
        out_shape=[
            jax.ShapeDtypeStruct((block_rows, span), kind),
            jax.ShapeDtypeStruct((dec_count, span), kind),
        ],
        in_specs=[band(width)] * m + [whole(d) for d in dec_ctxs] + [whole(w) for w in outs_w],
        out_specs=[band(span), pl.BlockSpec((dec_count, span), lambda i: (0, 0))],
        compiler_params=pltpu.CompilerParams(vmem_limit_bytes=BIG),
        name="out_proj",
    )(*pre_ctxs, *dec_ctxs, *outs_w)
    if n_tp != 2:
        dec_out = lax.psum_scatter(dec_out, "tp", scatter_dimension=1, tiled=True).astype(BF16)
        pre_out = lax.psum_scatter(pre_out, "tp", scatter_dimension=1, tiled=True).astype(BF16)
    return (dec_out, pre_out)


def solution(mesh):
    placed = (
        P("req", "tp"),
        P("req", "tp"),
        P(None, None, "tp", None),
        P("tp", None, None),
        P("req", None, "tp", None, None),
        P("req", None, "tp", None, None),
        P("req", None),
        P("req"),
        P(),
        P(),
        P("req"),
    )
    return jax.shard_map(
        functools.partial(local, mesh.shape["req"], mesh.shape["tp"]),
        mesh=mesh,
        in_specs=placed,
        out_specs=(P("req", "tp"), P("req", "tp")),
        check_vma=False,
    )
```

time: 312 us -> 112 us (0.36)
  blocking collectives: 86.9 us -> 0 us
  Pallas kernels: 0 us -> 85.7 us
  local copies, waits for them, and re-layouts: 68.5 us -> 9.1 us
  waiting for transfers between devices: 50.8 us -> 2.36 us
  matrix products: 41.4 us -> 0 us
  other arithmetic: 44.1 us -> 4.92 us
  between operations: 19.2 us -> 1.38 us
  starting transfers between devices: 0.17 us -> 6.72 us
    pallas_call x0 -> x8, Pallas kernels: none -> 85.7 us  [the longest x2 27.4 us: gather_all(): pl.pallas_call(functools.partial(gather_kernel, axis, count), out_shape=j...]
    unnamed x1 -> x0, blocking collectives: 58.9 us -> none
    reduce_scatter x3 -> x0, waiting for transfers between devices: 50.2 us -> none  [the longest x1 50.2 us: local(): lax.psum_scatter(pre_terms, 'tp', scatter_dimension=1, tiled=True)]
    dot_general x9 -> x0, matrix products: 41.4 us -> none  [the longest x1 11.1 us: local(): pre_terms = jnp.dot(pre_flat, flat_out, preferred_element_type=jnp.float32)]
    all_gather x2 -> x0, blocking collectives: 28 us -> none  [the longest x1 22.4 us: local(): all_queries = lax.all_gather(dec_query, 'req', axis=0, tiled=True)]
    sub x3 -> x1, other arithmetic: 23.4 us -> 0.66 us  [local(): begin = jnp.cumsum(group_sizes) - group_sizes]
    gather x3 -> x2, local copies, waits for them, and re-layouts: 16 us -> 2.02 us  [local(): padded[begin[:, None] + slot_at]]
    slice x3 -> x0, local copies, waits for them, and re-layouts: 10.8 us -> none  [the longest x1 6.8 us: local(): prefix_keys = prefix_cache[0, :, :, 0]]
  transfers between devices with their start and end apart: 4 -> 5, of which waited for: 1 -> 1; matrix products, arithmetic and copies ran while one was open for 34% -> 11% of each run, Pallas kernels for 0% -> 73%
where the time goes in v1:
time: 112 us; the launch traced here: 110 us
  Pallas kernels  85.7 us (77%)
  local copies, waits for them, and re-layouts  9.1 us (8%)
  starting transfers between devices  6.72 us (6%)
  other arithmetic  4.92 us (4%)
  waiting for transfers between devices  2.36 us (2%)
  between operations  1.38 us (1%)
    pallas_call x2, Pallas kernels, gather_all(): pl.pallas_call(functools.partial(gather_kernel, axis, count), out_shape=j...  27.4 us
    pallas_call x1, Pallas kernels, local(): pl.pallas_call(functools.partial(prefill_kernel, n, heads, chunk, scale),...  21.3 us
    pallas_call x1, Pallas kernels, prep(): pl.pallas_call(functools.partial(prep_kernel, groups, tokens), grid=(step...  16.9 us
    pallas_call x1, Pallas kernels, local(): pl.pallas_call(functools.partial(dec_attn_kernel, heads, scale), out_shap...  7.96 us
    pallas_call x1, Pallas kernels, local(): pl.pallas_call(functools.partial(out_kernel, m), grid=(block_rows // chun...  5.4 us
    pallas_call x1, Pallas kernels, local(): pl.pallas_call(functools.partial(dec_qkv_kernel, n, heads), out_shape=[ro...  4.53 us
    ppermute x1, starting transfers between devices, local(): dec_parts = [decode_tokens, lax.ppermute(decode_tokens, 'tp', swap)]  3.03 us
    unnamed x17, local copies, waits for them, and re-layouts  2.44 us
  transfers between devices with their start and end apart: 5, of which 1 were waited for; matrix products, arithmetic and copies ran while one was open for 11% of the time, Pallas kernels for 73%

profile of v1, /device:TPU:0, one launch (start us, length us, event | category | flops | bytes accessed | tf_op | source)
XLA Modules:
  0.0 110.2 jit_solution(4419657400682749015)
XLA Ops:
  0.6 3.0 %collective-permute-start.2 = (bf16[8,1024]{1,0:T(8,128)(2,1)}, bf16[8,1024]{1,0:T(8,128)(2,1)S(1)}, u32[]{:S(2)}, u32[]{:S(2)}) collective-permute-start(bf16[8,1024]{1,0:T(8,128)(2,1)} %refs_0_.3), channel_id=1, source_target_pairs={{0,1},{1,0},{2,3},{3,2},{4,5},{5,4},{6,7},{7,6},{8,9},{9,8},{10,11... | collective-permute-start | bytes 49160 | tf_op jit(solution)/shard_map/ppermute | solution.py:311
  3.7 0.1 collective-permute-start
  3.8 0.7 copy.17
  4.5 0.1 reduce
  4.6 0.7 sub.8
  5.3 0.1 compare_select_fusion
  5.4 0.1 reshape.150
  6.1 1.0 fusion
  7.1 0.7 concatenate.24
  7.8 0.0 copy-start
  7.8 1.9 %gather_fusion = s32[256]{0:T(256)S(1)} fusion(s32[144]{0:T(256)S(1)} %concatenate.24, s32[1024]{0:T(1024)S(1)} %pad_clamp_fusion), kind=kCustom, calls=%fused_computation | custom fusion | bytes 3072 | tf_op jit(solution)/shard_map/gather | solution.py:337
  9.8 0.1 reshape.149
  9.8 0.6 pad_add_fusion.scal
  10.5 1.0 pad_maximum_fusion
  11.5 0.0 copy-done
  11.5 1.2 %constant_dynamic-slice_fusion = (bf16[512,1024]{1,0:T(8,128)(2,1)}, bf16[512,1024]{1,0:T(8,128)(2,1)S(1)}) fusion(bf16[512,2048]{1,0:T(8,128)(2,1)S(1)} %bitcast.21, s32[]{:T(128)S(6)} %select_n.38, s32[]{:T(128)S(6)} %select_n.33), kind=kLoop, calls=%fused_computation.16 | loop fusion | bytes 4194312 | tf_op jit(solution)/shard_map/dynamic_slice | solution.py:378
  12.6 0.0 copy-start.7
  12.6 16.9 %prep.1 = (bf16[2048,1536]{1,0:T(8,128)(2,1)}, bf16[2048,1024]{1,0:T(8,128)(2,1)}, bf16[2048,1024]{1,0:T(8,128)(2,1)}) custom-call(bf16[24576,128]{1,0:T(8,128)(2,1)} %bitcast.17, bf16[16384,128]{1,0:T(8,128)(2,1)} %bitcast.18, bf16[16384,128]{1,0:T(8,128)(2,1)} %bitcast.19), custom_call_target="tpu_custom_call" | custom-call | flops 2000000000 | bytes 29360128 | tf_op jit(solution)/shard_map/prep/pallas_call | solution.py:54
  29.5 0.0 copy-done.7
  29.6 0.1 fusion.2
  29.7 0.0 collective-permute-done.refs_1_
  29.7 2.0 %collective-permute-start.4 = (bf16[512,1024]{1,0:T(8,128)(2,1)S(1)}, bf16[512,1024]{1,0:T(8,128)(2,1)S(1)}, u32[]{:S(2)}, u32[]{:S(2)}) collective-permute-start(bf16[512,1024]{1,0:T(8,128)(2,1)S(1)} %get-tuple-element.23), channel_id=1, source_target_pairs={{0,1},{1,0},{2,3},{3,2},{4,5},{5,4},{6,7},{7,6},{8,9},{9,8},{10,11... | collective-permute-start | bytes 3145736 | tf_op jit(solution)/shard_map/ppermute | solution.py:377
  31.7 0.0 copy-start.5
  31.7 0.0 copy-start.6
  31.7 21.3 %prefill.1.refs_0_ = bf16[512,512]{1,0:T(8,128)(2,1)} custom-call(s32[3]{0:T(128)} %pad_add_fusion.scal, bf16[512,1024]{1,0:T(8,128)(2,1)} %refs_0_.2, bf16[512,1024]{1,0:T(8,128)(2,1)} %collective-permute-done.refs_1_, bf16[2048,1536]{1,0:T(8,128)(2,1)} %get-tuple-element.15.refs_2_, f32[512,128]{1,0:T(8,128)} %get-tuple-element.34.refs_3_, ...), custom_call_target="tpu_custom_call" | custom-call | flops 8000000000 | bytes 13000000 | tf_op jit(solution)/shard_map/prefill/pallas_call | solution.py:383
  53.0 0.1 collective-permute-start.1
  53.1 0.6 pad_add_fusion.1.offs
  53.6 0.7 pad_maximum_fusion.2
  54.3 0.0 copy-done.5
  54.3 0.1 fusion.1
  54.4 0.6 select_n.37.owners
  55.0 0.7 copy.18.members
  55.7 0.0 copy-done.6
  55.7 0.7 copy.19.table
  56.3 0.7 copy.20.lens
  57.0 0.0 collective-permute-done.2.refs_1_
  57.0 0.0 copy-start.3
  57.0 0.6 copy-done.3
  57.6 4.5 %dec_qkv.1 = (bf16[8,512]{1,0:T(8,128)(2,1)}, bf16[8,512]{1,0:T(8,128)(2,1)}, bf16[8,512]{1,0:T(8,128)(2,1)}) custom-call(s32[2]{0:T(128)} %pad_add_fusion.1.offs, bf16[8,1024]{1,0:T(8,128)(2,1)} %refs_0_.3, bf16[8,1024]{1,0:T(8,128)(2,1)} %copy-done.3, bf16[2048,1536]{1,0:T(8,128)(2,1)} %get-tuple-element.15.refs_2_, f32[8,128]{1,0:T(8,128)} %get-tuple-element.36.refs_3_, ...), custom_call_target="tpu_custom_call" | custom-call | tf_op jit(solution)/shard_map/dec_qkv/pallas_call | solution.py:344
  62.1 9.5 %gather_all.2 = bf16[16,8,512]{2,1,0:T(8,128)(2,1)} custom-call(bf16[8,512]{1,0:T(8,128)(2,1)} %get-tuple-element.17.x_ref.q), custom_call_target="tpu_custom_call" | custom-call | tf_op jit(solution)/shard_map/gather_all/pallas_call | solution.py:106
  71.7 8.0 %dec_attn.1 = (f32[16,640]{1,0:T(8,128)}, f32[8,640]{1,0:T(8,128)}) custom-call(bf16[128,512]{1,0:T(8,128)(2,1)} %bitcast.22, s32[16,1]{1,0:T(8,128)} %copy.18.members, bf16[2048,1024]{1,0:T(8,128)(2,1)} %get-tuple-element.16.refs_5_.prefix, bf16[8,512]{1,0:T(8,128)(2,1)} %get-tuple-element.17.x_ref.q, bf16[8,512]{1,0:T(8,128)(2,1)} %get-tuple-element.18.knew, ...), custom_call_target="tpu_custom_call" | custom-call | tf_op jit(solution)/shard_map/dec_attn/pallas_call | solution.py:353
  79.7 17.8 %gather_all.3 = f32[16,16,640]{2,1,0:T(8,128)} custom-call(f32[16,640]{1,0:T(8,128)} %get-tuple-element.21.x_ref), custom_call_target="tpu_custom_call" | custom-call | tf_op jit(solution)/shard_map/gather_all/pallas_call | solution.py:106
  97.5 2.3 %merge.1.refs_2_ = bf16[8,512]{1,0:T(8,128)(2,1)} custom-call(s32[1]{0:T(128)} %bitcast.7.base, f32[256,640]{1,0:T(8,128)} %bitcast.20, s32[1,256]{1,0:T(1,128)} %select_n.37.owners, f32[8,640]{1,0:T(8,128)} %get-tuple-element.22.near), custom_call_target="tpu_custom_call" | custom-call | tf_op jit(solution)/shard_map/merge/pallas_call | solution.py:365
  99.7 1.5 %collective-permute-start.3 = (bf16[8,512]{1,0:T(8,128)(2,1)}, bf16[8,512]{1,0:T(8,128)(2,1)S(1)}, u32[]{:S(2)}, u32[]{:S(2)}) collective-permute-start(bf16[8,512]{1,0:T(8,128)(2,1)} %merge.1.refs_2_), channel_id=1, source_target_pairs={{0,1},{1,0},{2,3},{3,2},{4,5},{5,4},{6,7},{7,6},{8,9},{9,8},{10,11... | collective-permute-start | bytes 24584 | tf_op jit(solution)/shard_map/ppermute | solution.py:400
  101.3 2.3 %collective-permute-done.3.refs_3_ = bf16[8,512]{1,0:T(8,128)(2,1)S(1)} collective-permute-done((bf16[8,512]{1,0:T(8,128)(2,1)}, bf16[8,512]{1,0:T(8,128)(2,1)S(1)}, u32[]{:S(2)}, u32[]{:S(2)}) %collective-permute-start.3) | collective-permute-done | bytes 8224 | tf_op jit(solution)/shard_map/ppermute | solution.py:400
  103.6 0.0 copy-start.4
  103.6 0.0 collective-permute-done.1.refs_1_
  103.6 0.0 copy-start.2
  103.6 0.0 collective-permute-done.4.refs_5_
  103.6 0.0 copy-start.1
  103.6 0.6 copy-done.4
  104.2 0.2 copy-done.2
  104.4 0.3 copy-done.1
  104.8 5.4 %out_proj.1 = (bf16[512,1024]{1,0:T(8,128)(2,1)}, bf16[8,1024]{1,0:T(8,128)(2,1)}) custom-call(bf16[512,512]{1,0:T(8,128)(2,1)} %prefill.1.refs_0_, bf16[512,512]{1,0:T(8,128)(2,1)} %copy-done.2, bf16[8,512]{1,0:T(8,128)(2,1)} %merge.1.refs_2_, bf16[8,512]{1,0:T(8,128)(2,1)} %copy-done.4, bf16[512,1024]{1,0:T(8,128)(2,1)} %get-tuple-element.26.refs_4_, ...), custom_call_target="tpu_custom_call" | custom-call | tf_op jit(solution)/shard_map/out_proj/pallas_call | solution.py:406
  (6 shorter events, 0.1 us)
Async XLA Ops:
  0.6 56.4 %collective-permute-start.2 = (bf16[8,1024]{1,0:T(8,128)(2,1)}, bf16[8,1024]{1,0:T(8,128)(2,1)S(1)}, u32[]{:S(2)}, u32[]{:S(2)}) collective-permute-start(bf16[8,1024]{1,0:T(8,128)(2,1)} %refs_0_.3), channel_id=1, source_target_pairs={{0,1},{1,0},{2,3},{3,2},{4,5},{5,4},{6,7},{7,6},{8,9},{9,8},{10,11... | collective-permute-start | bytes 49160 | tf_op jit(solution)/shard_map/ppermute | solution.py:311
  3.7 26.0 %collective-permute-start = (bf16[512,1024]{1,0:T(8,128)(2,1)}, bf16[512,1024]{1,0:T(8,128)(2,1)}, u32[]{:S(2)}, u32[]{:S(2)}) collective-permute-start(bf16[512,1024]{1,0:T(8,128)(2,1)} %refs_0_.2), channel_id=1, source_target_pairs={{0,1},{1,0},{2,3},{3,2},{4,5},{5,4},{6,7},{7,6},{8,9},{9,8},{10,11... | collective-permute-start | bytes 3145736 | tf_op jit(solution)/shard_map/ppermute | solution.py:312
  7.8 3.6 %copy-start = (bf16[4,128,2048]{2,1,0:T(8,128)(2,1)S(1)}, bf16[4,128,2048]{2,1,0:T(8,128)(2,1)}, u32[]{:S(2)}) copy-start(bf16[4,128,2048]{2,1,0:T(8,128)(2,1)} %param.14) | copy-start | bytes 6291460
  12.6 16.9 %copy-start.7 = (s32[8]{0:T(128)S(1)}, s32[8]{0:T(128)}, u32[]{:S(2)}) copy-start(s32[8]{0:T(128)} %param.18) | copy-start | bytes 100
  29.7 73.9 %collective-permute-start.4 = (bf16[512,1024]{1,0:T(8,128)(2,1)S(1)}, bf16[512,1024]{1,0:T(8,128)(2,1)S(1)}, u32[]{:S(2)}, u32[]{:S(2)}) collective-permute-start(bf16[512,1024]{1,0:T(8,128)(2,1)S(1)} %get-tuple-element.23), channel_id=1, source_target_pairs={{0,1},{1,0},{2,3},{3,2},{4,5},{5,4},{6,7},{7,6},{8,9},{9,8},{10,11... | collective-permute-start | bytes 3145736 | tf_op jit(solution)/shard_map/ppermute | solution.py:377
  31.7 22.6 %copy-start.5 = (s32[16]{0:T(128)S(1)}, s32[16]{0:T(128)}, u32[]{:S(2)}) copy-start(s32[16]{0:T(128)} %param.19) | copy-start | bytes 196
  31.7 24.0 %copy-start.6 = (s32[8,2]{0,1:T(2,128)S(1)}, s32[8,2]{0,1:T(2,128)}, u32[]{:S(2)}) copy-start(s32[8,2]{0,1:T(2,128)} %param.17) | copy-start | bytes 196
  53.0 50.6 %collective-permute-start.1 = (bf16[512,512]{1,0:T(8,128)(2,1)}, bf16[512,512]{1,0:T(8,128)(2,1)S(1)}, u32[]{:S(2)}, u32[]{:S(2)}) collective-permute-start(bf16[512,512]{1,0:T(8,128)(2,1)} %prefill.1.refs_0_), channel_id=1, source_target_pairs={{0,1},{1,0},{2,3},{3,2},{4,5},{5,4},{6,7},{7,6},{8,9},{9,8},{10,11... | collective-permute-start | bytes 1572872 | tf_op jit(solution)/shard_map/ppermute | solution.py:399
  57.0 0.6 copy-start.3
  99.7 3.9 %collective-permute-start.3 = (bf16[8,512]{1,0:T(8,128)(2,1)}, bf16[8,512]{1,0:T(8,128)(2,1)S(1)}, u32[]{:S(2)}, u32[]{:S(2)}) collective-permute-start(bf16[8,512]{1,0:T(8,128)(2,1)} %merge.1.refs_2_), channel_id=1, source_target_pairs={{0,1},{1,0},{2,3},{3,2},{4,5},{5,4},{6,7},{7,6},{8,9},{9,8},{10,11... | collective-permute-start | bytes 24584 | tf_op jit(solution)/shard_map/ppermute | solution.py:400
  103.6 0.6 copy-start.4
  103.6 0.8 copy-start.2
  103.6 1.2 %copy-start.1 = (bf16[512,1024]{1,0:T(8,128)(2,1)}, bf16[512,1024]{1,0:T(8,128)(2,1)S(1)}, u32[]{:S(2)}) copy-start(bf16[512,1024]{1,0:T(8,128)(2,1)S(1)} %collective-permute-done.4.refs_5_) | copy-start | bytes 3145732

commit v2 on v1

--- a/solution.py
+++ b/solution.py
@@ -9,6 +9,7 @@
 from jax.sharding import PartitionSpec as P
 
 GMAX = 16
+CHUNK = 128
 F32, BF16 = jnp.float32, jnp.bfloat16
 MESH = pl.DeviceIdType.MESH
 VM = pl.BlockSpec(memory_space=pltpu.VMEM)
@@ -273,6 +274,340 @@
     @pl.when(pl.program_id(0) == 0)
     def _():
         dec_out[...] = sum(dot(c[...], w[...]) for c, w in zip(decs, ws)).astype(dec_out.dtype)
+
+
+def fused_kernel(
+    n_req, heads, scale, own_dec, peer_dec, own_pre, peer_pre, w_hbm, prefix_hbm, pool_hbm,
+    wout_hbm, dcos, dsin, pcos, psin, sizes, order, table, lens, start,
+    dec_out, pre_out,
+    w_ref, own_v, peer_v, prefix, pool, wout_own, wout_peer, kself, vself, ctx_own, ctx_peer,
+    dctx_own, dctx_peer, myq, allq, qwide, far, farsend, farrecv, near,
+    local_sem, q_send, q_recv, f_send, f_recv, t_send, t_recv,
+):
+    me = lax.axis_index("req")
+    side = lax.axis_index("tp")
+    other = 1 - side
+    rows, share = own_dec.shape
+    block = own_pre.shape[0]
+    width = heads * 128
+    every = n_req * rows
+    mine = pl.ds(pl.multiple_of(side * share, 128), share)
+    theirs = pl.ds(pl.multiple_of(other * share, 128), share)
+    loads = [
+        pltpu.make_async_copy(a, b, local_sem.at[k])
+        for k, (a, b) in enumerate(
+            [
+                (w_hbm, w_ref),
+                (own_pre, own_v),
+                (peer_pre, peer_v),
+                (prefix_hbm, prefix),
+                (pool_hbm, pool),
+                (wout_hbm.at[:, mine], wout_own),
+            ]
+        )
+    ]
+    for one in loads:
+        one.start()
+    barrier = pltpu.get_barrier_semaphore()
+
+    def greet(k, _):
+        pl.semaphore_signal(
+            barrier, inc=1, device_id={"req": lax.rem(me + k, n_req)}, device_id_type=MESH
+        )
+        return 0
+
+    lax.fori_loop(1, n_req, greet, 0)
+    pl.semaphore_signal(barrier, inc=1, device_id={"tp": other}, device_id_type=MESH)
+    pl.semaphore_wait(barrier, n_req)
+
+    def swap(src, dst, k):
+        return pltpu.make_async_remote_copy(
+            src_ref=src,
+            dst_ref=dst,
+            send_sem=t_send.at[k],
+            recv_sem=t_recv.at[k],
+            device_id={"tp": other},
+            device_id_type=MESH,
+        )
+
+    weight_swap = swap(wout_hbm.at[:, theirs], wout_peer, 0)
+    weight_swap.start()
+
+    def q_copy(k):
+        return pltpu.make_async_remote_copy(
+            src_ref=myq,
+            dst_ref=allq.at[me],
+            send_sem=q_send.at[k],
+            recv_sem=q_recv.at[k],
+            device_id={"req": lax.rem(me + k, n_req)},
+            device_id_type=MESH,
+        )
+
+    def f_copy(k):
+        to = lax.rem(me + k, n_req)
+        return pltpu.make_async_remote_copy(
+            src_ref=farsend.at[to],
+            dst_ref=farrecv.at[me],
+            send_sem=f_send.at[k],
+            recv_sem=f_recv.at[k],
+            device_id={"req": to},
+            device_id_type=MESH,
+        )
+
+    def start_all(make):
+        def go(k, _):
+            make(k).start()
+            return 0
+
+        lax.fori_loop(1, n_req, go, 0)
+
+    def wait_all(make):
+        def go(k, _):
+            make(k).wait()
+            return 0
+
+        lax.fori_loop(1, n_req, go, 0)
+
+    offs = [side * share, other * share]
+
+    loads[0].wait()
+    y = qkv_rows([own_dec[...], peer_dec[...]], offs, w_ref)
+    c, s = dcos[...], dsin[...]
+    dq, dk, dv = [], [], []
+    for h in range(heads):
+        dq.append(turn(y[:, h * 128 : (h + 1) * 128], c, s).astype(BF16))
+        dk.append(
+            turn(y[:, (heads + h) * 128 : (heads + h + 1) * 128], c, s).astype(BF16).astype(F32)
+        )
+        dv.append(
+            y[:, (2 * heads + h) * 128 : (2 * heads + h + 1) * 128].astype(BF16).astype(F32)
+        )
+    for h in range(heads):
+        myq[:, h * 128 : (h + 1) * 128] = dq[h]
+    start_all(q_copy)
+    allq[me] = myq[...]
+
+    lane = lax.broadcasted_iota(jnp.int32, (rows, 128), 1)
+    row = lax.broadcasted_iota(jnp.int32, (rows, 128), 0)
+    loads[4].wait()
+    slots = pool.shape[0]
+    t = lax.broadcasted_iota(jnp.int32, (rows, slots), 1)
+    page, off = lax.shift_right_logical(t, 7), t & 127
+    span = jnp.zeros((rows, 128), jnp.int32)
+    for r in range(rows):
+        span = jnp.where(row == r, lens[r], span)
+    valid = None
+    for j in range(table.shape[0]):
+        held = jnp.zeros((rows, 128), jnp.int32)
+        for r in range(rows):
+            held = jnp.where(row == r, table[j, r], held)
+        one = (page == held[:, :1]) & (off + j * 128 < span[:, :1])
+        valid = one if valid is None else valid | one
+    stat = jnp.zeros((rows, 128), F32)
+    for h in range(heads):
+        here = slice(h * 128, (h + 1) * 128)
+        kcol = slice(h * 256, h * 256 + 128)
+        vcol = slice(h * 256 + 128, h * 256 + 256)
+        sc = jnp.where(valid, dot_t(dq[h], pool[:, kcol]) * scale, -1e30)
+        own = jnp.sum(dq[h].astype(F32) * dk[h], axis=1, keepdims=True) * scale
+        m = jnp.maximum(jnp.max(sc, axis=1, keepdims=True), own)
+        w = jnp.where(valid, jnp.exp(sc - m), 0.0)
+        ow = jnp.exp(own - m)
+        stat = jnp.where(lane == h, m, stat)
+        stat = jnp.where(lane == heads + h, jnp.sum(w, axis=1, keepdims=True) + ow, stat)
+        near[:, here] = dot(w.astype(BF16), pool[:, vcol]) + ow.astype(BF16).astype(F32) * dv[h]
+    near[:, width:] = stat
+
+    chunk = CHUNK
+    far_len = prefix.shape[0]
+    bias = jnp.where(
+        lax.broadcasted_iota(jnp.int32, (1, far_len), 1) < start[0], 0.0, -1e30
+    )
+    low = lax.broadcasted_iota(jnp.int32, (chunk, chunk), 1) <= lax.broadcasted_iota(
+        jnp.int32, (chunk, chunk), 0
+    )
+    factor = scale * math.log2(math.e)
+
+    def band(k):
+        return slice(k * chunk, (k + 1) * chunk)
+
+    def ctx_swap(k):
+        return swap(ctx_own.at[band(k)], ctx_peer.at[band(k)], 2 + k)
+
+    def prefill(k):
+        at = band(k)
+        y = qkv_rows([own_v[at, :], peer_v[at, :]], offs, w_ref)
+        c, s = pcos[at, :], psin[at, :]
+        for h in range(heads):
+            here = slice(h * 128, (h + 1) * 128)
+            kcol = slice(h * 256, h * 256 + 128)
+            vcol = slice(h * 256 + 128, h * 256 + 256)
+            qh = turn(y[:, h * 128 : (h + 1) * 128], c, s).astype(BF16)
+            kh = turn(y[:, (heads + h) * 128 : (heads + h + 1) * 128], c, s).astype(BF16)
+            vh = y[:, (2 * heads + h) * 128 : (2 * heads + h + 1) * 128].astype(BF16)
+            kself[at, here] = kh
+            vself[at, here] = vh
+            pieces = [(dot_t(qh, prefix[:, kcol]) + bias, prefix, vcol, slice(0, far_len))]
+            if k:
+                back = slice(0, k * chunk)
+                pieces.append((dot_t(qh, kself[back, here]), vself, here, back))
+            tip = jnp.where(low, dot_t(qh, kh), -1e30)
+            m = jnp.max(tip, axis=1, keepdims=True)
+            for sc, _, _, _ in pieces:
+                m = jnp.maximum(m, jnp.max(sc, axis=1, keepdims=True))
+            w = jnp.exp2((tip - m) * factor)
+            l = jnp.sum(w, axis=1, keepdims=True)
+            o = dot(w.astype(BF16), vh)
+            for sc, ref, cols, part in pieces:
+                w = jnp.exp2((sc - m) * factor)
+                l = l + jnp.sum(w, axis=1, keepdims=True)
+                o = o + dot(w.astype(BF16), ref[part, cols])
+            ctx_own[at, here] = (o / l).astype(BF16)
+        ctx_swap(k).start()
+
+    loads[1].wait()
+    loads[2].wait()
+    loads[3].wait()
+    prefill(0)
+
+    wait_all(q_copy)
+    for g in range(n_req):
+        qwide[g * rows : (g + 1) * rows, :] = allq[g].astype(F32)
+    begin, size = jnp.int32(0), jnp.int32(0)
+    for g in range(n_req):
+        begin = begin + jnp.where(g < me, sizes[g], 0)
+        size = size + jnp.where(g == me, sizes[g], 0)
+    slot = lax.broadcasted_iota(jnp.int32, (GMAX, every), 0)
+    rank = lax.broadcasted_iota(jnp.int32, (GMAX, every), 1)
+    held = jnp.where((rank == begin + slot) & (slot < size), 1.0, 0.0).astype(BF16)
+    named = jnp.where(
+        order[...] == lax.broadcasted_iota(jnp.int32, (every, every), 0), 1.0, 0.0
+    ).astype(BF16)
+    pick = dot_t(held, named).astype(BF16)
+    back = dot_t(named, held)
+    chosen = dot(pick, qwide[...].astype(BF16)).astype(BF16)
+    lane = lax.broadcasted_iota(jnp.int32, (GMAX, 128), 1)
+    stat = jnp.zeros((GMAX, 128), F32)
+    for h in range(heads):
+        here = slice(h * 128, (h + 1) * 128)
+        kcol = slice(h * 256, h * 256 + 128)
+        vcol = slice(h * 256 + 128, h * 256 + 256)
+        sc = dot_t(chosen[:, here], prefix[:, kcol]) * scale
+        m = jnp.max(sc, axis=1, keepdims=True)
+        w = jnp.exp(sc - m)
+        stat = jnp.where(lane == h, m, stat)
+        stat = jnp.where(lane == heads + h, jnp.sum(w, axis=1, keepdims=True), stat)
+        far[:, here] = dot(w.astype(BF16), prefix[:, vcol])
+    far[:, width:] = stat
+    spread = jnp.dot(
+        back, far[...], preferred_element_type=F32, precision=lax.Precision.HIGHEST
+    )
+    for g in range(n_req):
+        farsend[g] = spread[g * rows : (g + 1) * rows, :]
+    start_all(f_copy)
+    farrecv[me] = farsend[me]
+
+    count = block // chunk
+    for k in range(1, count - 1):
+        prefill(k)
+
+    wait_all(f_copy)
+    got = farrecv[0]
+    for g in range(1, n_req):
+        got = got + farrecv[g]
+    for h in range(heads):
+        here = slice(h * 128, (h + 1) * 128)
+        mp, lp = got[:, width + h : width + h + 1], got[:, width + heads + h : width + heads + h + 1]
+        ml = near[:, width + h : width + h + 1]
+        ll = near[:, width + heads + h : width + heads + h + 1]
+        top = jnp.maximum(mp, ml)
+        a, b = jnp.exp(mp - top), jnp.exp(ml - top)
+        dctx_own[:, here] = ((a * got[:, here] + b * near[:, here]) / (a * lp + b * ll)).astype(BF16)
+    dec_swap = swap(dctx_own, dctx_peer, 1)
+    dec_swap.start()
+    prefill(count - 1)
+
+    loads[5].wait()
+    weight_swap.wait()
+    dec_swap.wait()
+    dec_out[...] = (
+        dot(dctx_own[...], wout_own[...]) + dot(dctx_peer[...], wout_peer[...])
+    ).astype(BF16)
+    for k in range(count):
+        ctx_swap(k).wait()
+        at = band(k)
+        pre_out[at, :] = (
+            dot(ctx_own[at, :], wout_own[...]) + dot(ctx_peer[at, :], wout_peer[...])
+        ).astype(BF16)
+
+
+def places_tables(places):
+    lane = jnp.arange(128, dtype=jnp.int32)
+    inverse = 10000.0 ** (-((lane & 63).astype(F32) / 64))
+    angles = places.astype(F32)[:, None] * inverse[None, :]
+    return jnp.cos(angles), jnp.sin(angles) * jnp.where(lane < 64, -1.0, 1.0)[None, :]
+
+
+def fused(
+    n_req, own_dec, peer_dec, own_pre, peer_pre, weight, prefix, pool, flat_out,
+    group_sizes, member_order, page_table, cached_len, span_start,
+):
+    rows, share = own_dec.shape
+    block = own_pre.shape[0]
+    width = flat_out.shape[0]
+    heads = width // 128
+    every = n_req * rows
+    dcos, dsin = places_tables(prefix.shape[0] + cached_len)
+    pcos, psin = places_tables(span_start[0] + jnp.arange(block, dtype=jnp.int32))
+    anyw = pl.BlockSpec(memory_space=pl.ANY)
+    dma = pltpu.SemaphoreType.DMA
+    count = block // CHUNK
+    return pl.pallas_call(
+        functools.partial(fused_kernel, n_req, heads, 128 ** (-0.5)),
+        out_shape=[
+            jax.ShapeDtypeStruct((rows, share), BF16),
+            jax.ShapeDtypeStruct((block, share), BF16),
+        ],
+        in_specs=[VM, VM] + [anyw] * 6 + [VM] * 4 + [SM, VM, SM, SM, SM],
+        out_specs=[VM, VM],
+        scratch_shapes=[
+            pltpu.VMEM(weight.shape, BF16),
+            pltpu.VMEM((block, share), BF16),
+            pltpu.VMEM((block, share), BF16),
+            pltpu.VMEM(prefix.shape, BF16),
+            pltpu.VMEM(pool.shape, BF16),
+            pltpu.VMEM((width, share), BF16),
+            pltpu.VMEM((width, share), BF16),
+            pltpu.VMEM((block, width), BF16),
+            pltpu.VMEM((block, width), BF16),
+            pltpu.VMEM((block, width), BF16),
+            pltpu.VMEM((block, width), BF16),
+            pltpu.VMEM((rows, width), BF16),
+            pltpu.VMEM((rows, width), BF16),
+            pltpu.VMEM((rows, width), BF16),
+            pltpu.VMEM((n_req, rows, width), BF16),
+            pltpu.VMEM((every, width), F32),
+            pltpu.VMEM((GMAX, width + 128), F32),
+            pltpu.VMEM((n_req, rows, width + 128), F32),
+            pltpu.VMEM((n_req, rows, width + 128), F32),
+            pltpu.VMEM((rows, width + 128), F32),
+            dma((6,)),
+            dma((n_req,)),
+            dma((n_req,)),
+            dma((n_req,)),
+            dma((n_req,)),
+            dma((2 + count,)),
+            dma((2 + count,)),
+        ],
+        compiler_params=pltpu.CompilerParams(
+            collective_id=3, has_side_effects=True, vmem_limit_bytes=BIG
+        ),
+        name="fused",
+    )(
+        own_dec, peer_dec, own_pre, peer_pre, weight, prefix, pool, flat_out,
+        dcos, dsin, pcos, psin, group_sizes, member_order[None, :], page_table.T, cached_len,
+        span_start,
+    )
 
 
 def tables(places):
@@ -330,6 +665,13 @@
         + prep([prefix_cache.reshape(-1, 128)], [2 * heads], prefix_len)
         + prep([page_pool.reshape(-1, 128)], [2 * heads], slots)
     )
+    if n_tp == 2 and block_rows % CHUNK == 0 and block_rows > CHUNK:
+        dec_out, pre_out = fused(
+            n_req, *dec_parts, *pre_parts, weight, prefix, pool,
+            out_weight.reshape(width, out_weight.shape[2]),
+            group_sizes, member_order, page_table, cached_len, span_start,
+        )
+        return (dec_out, pre_out)
     begin = jnp.cumsum(group_sizes) - group_sizes
     slot_at = jnp.arange(GMAX, dtype=jnp.int32)[None, :]
     padded = jnp.concatenate([member_order, jnp.zeros((GMAX,), jnp.int32)])

time: 112 us -> 77.3 us (0.69); the launches traced: 110 us -> 76.6 us
  Pallas kernels: 85.7 us -> 60.5 us
  local copies, waits for them, and re-layouts: 9.1 us -> 4.56 us
  starting transfers between devices: 6.72 us -> 3.11 us
  other arithmetic: 4.92 us -> 3.19 us
  waiting for transfers between devices: 2.36 us -> 4.02 us
    pallas_call x7 -> x1, Pallas kernels: 68.8 us -> 43.6 us  [fused(): pl.pallas_call(functools.partial(fused_kernel, n_req, heads, 128 ** (-0.5...]
    ppermute x1, waiting for transfers between devices: 0.01 us -> 4.02 us  [local(): pre_parts = [prefill_tokens, lax.ppermute(prefill_tokens, 'tp', swap)]]
    ppermute x3 -> x0, starting transfers between devices: 3.61 us -> none  [the longest x1 2 us: local(): peer_w = lax.ppermute(theirs, 'tp', swap)]
    mul x0 -> x2, other arithmetic: none -> 2.51 us  [places_tables(): jnp.sin(angles) * jnp.where(lane < 64, -1.0, 1.0)[None, :]]
    ppermute x3 -> x0, waiting for transfers between devices: 2.35 us -> none  [the longest x1 2.35 us: local(): dec_ctxs = [dec_ctx, lax.ppermute(dec_ctx, 'tp', swap)]]
    concatenate x3 -> x0, other arithmetic: 2.28 us -> none  [the longest x2 1.66 us: tables(): return (jnp.concatenate([c, c], axis=1), jnp.concatenate([-s, s], axis=1))]
    unnamed x17 -> x6, local copies, waits for them, and re-layouts: 2.44 us -> 4.56 us
    gather x2 -> x0, local copies, waits for them, and re-layouts: 2.02 us -> none  [local(): padded[begin[:, None] + slot_at]]
  transfers between devices with their start and end apart: 5 -> 2, of which waited for: 1 -> 1; matrix products, arithmetic and copies ran while one was open for 11% -> 4% of each run, Pallas kernels for 73% -> 22%
where the time goes in v2:
time: 77.3 us; the launch traced here: 76.6 us
  Pallas kernels  60.5 us (78%)
  local copies, waits for them, and re-layouts  4.56 us (6%)
  waiting for transfers between devices  4.02 us (5%)
  other arithmetic  3.19 us (4%)
  starting transfers between devices  3.11 us (4%)
  between operations  1.31 us (2%)
    pallas_call x1, Pallas kernels, fused(): pl.pallas_call(functools.partial(fused_kernel, n_req, heads, 128 ** (-0.5...  43.6 us
    pallas_call x1, Pallas kernels, prep(): pl.pallas_call(functools.partial(prep_kernel, groups, tokens), grid=(step...  16.9 us
    unnamed x6, local copies, waits for them, and re-layouts  4.56 us
    ppermute x1, waiting for transfers between devices, local(): pre_parts = [prefill_tokens, lax.ppermute(prefill_tokens, 'tp', swap)]  4.02 us
    ppermute x1, starting transfers between devices, local(): dec_parts = [decode_tokens, lax.ppermute(decode_tokens, 'tp', swap)]  3.03 us
    mul x2, other arithmetic, places_tables(): jnp.sin(angles) * jnp.where(lane < 64, -1.0, 1.0)[None, :]  2.51 us
  transfers between devices with their start and end apart: 2, of which 1 were waited for; matrix products, arithmetic and copies ran while one was open for 4% of the time, Pallas kernels for 22%

profile of v2, /device:TPU:0, one launch (start us, length us, event | category | flops | bytes accessed | tf_op | source)
XLA Modules:
  0.0 76.6 jit_solution(5825158438084876609)
XLA Ops:
  0.6 3.0 %collective-permute-start = (bf16[8,1024]{1,0:T(8,128)(2,1)}, bf16[8,1024]{1,0:T(8,128)(2,1)S(1)}, u32[]{:S(2)}, u32[]{:S(2)}) collective-permute-start(bf16[8,1024]{1,0:T(8,128)(2,1)} %own_dec.1), channel_id=1, source_target_pairs={{0,1},{1,0},{2,3},{3,2},{4,5},{5,4},{6,7},{7,6},{8,9},{9,8},{10,11... | collective-permute-start | bytes 49160 | tf_op jit(solution)/shard_map/ppermute | solution.py:646
  3.7 0.1 collective-permute-start.1
  4.4 0.7 add_convert_fusion.1
  5.1 0.7 fusion.1
  5.8 1.8 %fusion = (f32[512,128]{1,0:T(8,128)}, f32[512,128]{1,0:T(8,128)}) fusion(f32[128]{0:T(128)S(1)} %get-tuple-element.12, f32[128]{0:T(128)S(1)} %get-tuple-element.13, f32[512]{0:T(512)S(1)} %add_convert_fusion), kind=kLoop, calls=%fused_computation.2 | loop fusion | flops 131072 | bytes 527360 | tf_op jit(solution)/shard_map/mul | solution.py:548
  7.6 16.9 %prep.1 = (bf16[2048,1536]{1,0:T(8,128)(2,1)}, bf16[2048,1024]{1,0:T(8,128)(2,1)}, bf16[2048,1024]{1,0:T(8,128)(2,1)}) custom-call(bf16[24576,128]{1,0:T(8,128)(2,1)} %bitcast.8, bf16[16384,128]{1,0:T(8,128)(2,1)} %bitcast.9, bf16[16384,128]{1,0:T(8,128)(2,1)} %bitcast.10), custom_call_target="tpu_custom_call" | custom-call | flops 2000000000 | bytes 29360128 | tf_op jit(solution)/shard_map/prep/pallas_call | solution.py:55
  24.5 0.0 collective-permute-done.peer_dec
  24.5 0.0 copy-start.1
  24.5 4.0 %collective-permute-done.1.peer_pre = bf16[512,1024]{1,0:T(8,128)(2,1)S(1)} collective-permute-done((bf16[512,1024]{1,0:T(8,128)(2,1)}, bf16[512,1024]{1,0:T(8,128)(2,1)S(1)}, u32[]{:S(2)}, u32[]{:S(2)}) %collective-permute-start.1) | collective-permute-done | bytes 1048608 | tf_op jit(solution)/shard_map/ppermute | solution.py:647
  28.5 0.0 copy-start
  28.5 0.0 copy-done.1
  28.5 1.0 %copy-done = bf16[512,1024]{1,0:T(8,128)(2,1)} copy-done((bf16[512,1024]{1,0:T(8,128)(2,1)}, bf16[512,1024]{1,0:T(8,128)(2,1)S(1)}, u32[]{:S(2)}) %copy-start) | copy-done | bytes 1048600
  29.5 43.6 %fused.1 = (bf16[8,1024]{1,0:T(8,128)(2,1)}, bf16[512,1024]{1,0:T(8,128)(2,1)}) custom-call(bf16[8,1024]{1,0:T(8,128)(2,1)} %own_dec.1, bf16[8,1024]{1,0:T(8,128)(2,1)} %copy-done.1, bf16[512,1024]{1,0:T(8,128)(2,1)} %own_pre.1, bf16[512,1024]{1,0:T(8,128)(2,1)} %copy-done, bf16[2048,1536]{1,0:T(8,128)(2,1)} %get-tuple-element.5.w_hbm, ...), custom_call_target="tpu_custom_call" | custom-call | tf_op jit(solution)/shard_map/fused/pallas_call | solution.py:565
  73.1 1.3 %copy.16 = bf16[8,1024]{1,0:T(8,128)(2,1)} copy(bf16[8,1024]{1,0:T(8,128)(2,1)} %get-tuple-element.16) | data formatting | bytes 32768
  74.4 2.3 %copy.17 = bf16[512,1024]{1,0:T(8,128)(2,1)} copy(bf16[512,1024]{1,0:T(8,128)(2,1)} %get-tuple-element.17) | data formatting | bytes 2097152
  (2 shorter events, 0.0 us)
Async XLA Ops:
  0.6 23.8 %collective-permute-start = (bf16[8,1024]{1,0:T(8,128)(2,1)}, bf16[8,1024]{1,0:T(8,128)(2,1)S(1)}, u32[]{:S(2)}, u32[]{:S(2)}) collective-permute-start(bf16[8,1024]{1,0:T(8,128)(2,1)} %own_dec.1), channel_id=1, source_target_pairs={{0,1},{1,0},{2,3},{3,2},{4,5},{5,4},{6,7},{7,6},{8,9},{9,8},{10,11... | collective-permute-start | bytes 49160 | tf_op jit(solution)/shard_map/ppermute | solution.py:646
  3.7 24.8 %collective-permute-start.1 = (bf16[512,1024]{1,0:T(8,128)(2,1)}, bf16[512,1024]{1,0:T(8,128)(2,1)S(1)}, u32[]{:S(2)}, u32[]{:S(2)}) collective-permute-start(bf16[512,1024]{1,0:T(8,128)(2,1)} %own_pre.1), channel_id=1, source_target_pairs={{0,1},{1,0},{2,3},{3,2},{4,5},{5,4},{6,7},{7,6},{8,9},{9,8},{10,11... | collective-permute-start | bytes 3145736 | tf_op jit(solution)/shard_map/ppermute | solution.py:647
  24.5 4.0 %copy-start.1 = (bf16[8,1024]{1,0:T(8,128)(2,1)}, bf16[8,1024]{1,0:T(8,128)(2,1)S(1)}, u32[]{:S(2)}) copy-start(bf16[8,1024]{1,0:T(8,128)(2,1)S(1)} %collective-permute-done.peer_dec) | copy-start | bytes 49156
  28.5 1.0 %copy-start = (bf16[512,1024]{1,0:T(8,128)(2,1)}, bf16[512,1024]{1,0:T(8,128)(2,1)S(1)}, u32[]{:S(2)}) copy-start(bf16[512,1024]{1,0:T(8,128)(2,1)S(1)} %collective-permute-done.1.peer_pre) | copy-start | bytes 3145732

commit v3 on v2

--- a/solution.py
+++ b/solution.py
@@ -277,10 +277,10 @@
 
 
 def fused_kernel(
-    n_req, heads, scale, own_dec, peer_dec, own_pre, peer_pre, w_hbm, prefix_hbm, pool_hbm,
+    n_req, heads, scale, own_dec, own_pre, peer_pre, w_hbm, prefix_hbm, pool_hbm,
     wout_hbm, dcos, dsin, pcos, psin, sizes, order, table, lens, start,
     dec_out, pre_out,
-    w_ref, own_v, peer_v, prefix, pool, wout_own, wout_peer, kself, vself, ctx_own, ctx_peer,
+    peer_dec, w_ref, own_v, peer_v, prefix, pool, wout_own, wout_peer, kself, vself, ctx_own, ctx_peer,
     dctx_own, dctx_peer, myq, allq, qwide, far, farsend, farrecv, near,
     local_sem, q_send, q_recv, f_send, f_recv, t_send, t_recv,
 ):
@@ -299,7 +299,7 @@
             [
                 (w_hbm, w_ref),
                 (own_pre, own_v),
-                (peer_pre, peer_v),
+                (peer_pre, peer_v.at[: peer_pre.shape[0]]),
                 (prefix_hbm, prefix),
                 (pool_hbm, pool),
                 (wout_hbm.at[:, mine], wout_own),
@@ -330,6 +330,12 @@
             device_id_type=MESH,
         )
 
+    count = block // CHUNK
+    dec_tokens_swap = swap(own_dec, peer_dec, 2 + count)
+    dec_tokens_swap.start()
+    last = slice(peer_pre.shape[0], block)
+    last_swap = swap(own_pre.at[last], peer_v.at[last], 3 + count)
+    last_swap.start()
     weight_swap = swap(wout_hbm.at[:, theirs], wout_peer, 0)
     weight_swap.start()
 
@@ -371,6 +377,7 @@
     offs = [side * share, other * share]
 
     loads[0].wait()
+    dec_tokens_swap.wait()
     y = qkv_rows([own_dec[...], peer_dec[...]], offs, w_ref)
     c, s = dcos[...], dsin[...]
     dq, dk, dv = [], [], []
@@ -507,7 +514,6 @@
     start_all(f_copy)
     farrecv[me] = farsend[me]
 
-    count = block // chunk
     for k in range(1, count - 1):
         prefill(k)
 
@@ -525,6 +531,7 @@
         dctx_own[:, here] = ((a * got[:, here] + b * near[:, here]) / (a * lp + b * ll)).astype(BF16)
     dec_swap = swap(dctx_own, dctx_peer, 1)
     dec_swap.start()
+    last_swap.wait()
     prefill(count - 1)
 
     loads[5].wait()
@@ -549,7 +556,7 @@
 
 
 def fused(
-    n_req, own_dec, peer_dec, own_pre, peer_pre, weight, prefix, pool, flat_out,
+    n_req, own_dec, own_pre, peer_pre, weight, prefix, pool, flat_out,
     group_sizes, member_order, page_table, cached_len, span_start,
 ):
     rows, share = own_dec.shape
@@ -568,9 +575,10 @@
             jax.ShapeDtypeStruct((rows, share), BF16),
             jax.ShapeDtypeStruct((block, share), BF16),
         ],
-        in_specs=[VM, VM] + [anyw] * 6 + [VM] * 4 + [SM, VM, SM, SM, SM],
+        in_specs=[VM] + [anyw] * 6 + [VM] * 4 + [SM, VM, SM, SM, SM],
         out_specs=[VM, VM],
         scratch_shapes=[
+            pltpu.VMEM((rows, share), BF16),
             pltpu.VMEM(weight.shape, BF16),
             pltpu.VMEM((block, share), BF16),
             pltpu.VMEM((block, share), BF16),
@@ -596,15 +604,15 @@
             dma((n_req,)),
             dma((n_req,)),
             dma((n_req,)),
-            dma((2 + count,)),
-            dma((2 + count,)),
+            dma((4 + count,)),
+            dma((4 + count,)),
         ],
         compiler_params=pltpu.CompilerParams(
             collective_id=3, has_side_effects=True, vmem_limit_bytes=BIG
         ),
         name="fused",
     )(
-        own_dec, peer_dec, own_pre, peer_pre, weight, prefix, pool, flat_out,
+        own_dec, own_pre, peer_pre, weight, prefix, pool, flat_out,
         dcos, dsin, pcos, psin, group_sizes, member_order[None, :], page_table.T, cached_len,
         span_start,
     )
@@ -642,7 +650,12 @@
     me = lax.axis_index("req")
     side = lax.axis_index("tp")
     swap = [(0, 1), (1, 0)]
-    if n_tp == 2:
+    joined = n_tp == 2 and block_rows % CHUNK == 0 and block_rows > CHUNK
+    if joined:
+        head = prefill_tokens[: block_rows - CHUNK]
+        head = lax.ppermute(head, "tp", swap)
+        offs = [side * share, (1 - side) * share]
+    elif n_tp == 2:
         dec_parts = [decode_tokens, lax.ppermute(decode_tokens, "tp", swap)]
         pre_parts = [prefill_tokens, lax.ppermute(prefill_tokens, "tp", swap)]
         offs = [side * share, (1 - side) * share]
@@ -665,9 +678,9 @@
         + prep([prefix_cache.reshape(-1, 128)], [2 * heads], prefix_len)
         + prep([page_pool.reshape(-1, 128)], [2 * heads], slots)
     )
-    if n_tp == 2 and block_rows % CHUNK == 0 and block_rows > CHUNK:
+    if joined:
         dec_out, pre_out = fused(
-            n_req, *dec_parts, *pre_parts, weight, prefix, pool,
+            n_req, decode_tokens, prefill_tokens, head, weight, prefix, pool,
             out_weight.reshape(width, out_weight.shape[2]),
             group_sizes, member_order, page_table, cached_len, span_start,
         )

time: 77.3 us -> 79.3 us (1.026)
  Pallas kernels: 60.5 us -> 66.1 us
  waiting for transfers between devices: 4.02 us -> 0.01 us
  local copies, waits for them, and re-layouts: 4.56 us -> 5.66 us
    pallas_call x1, Pallas kernels: 43.6 us -> 49.2 us  [fused(): pl.pallas_call(functools.partial(fused_kernel, n_req, heads, 128 ** (-0.5...]
    ppermute x2 -> x1, waiting for transfers between devices: 4.02 us -> 0.01 us  [local(): head = lax.ppermute(head, 'tp', swap)]
    slice x0 -> x1, local copies, waits for them, and re-layouts: none -> 1.19 us  [local(): head = prefill_tokens[:block_rows - CHUNK]]
    ppermute x2 -> x1, starting transfers between devices: 3.11 us -> 3.03 us  [local(): head = lax.ppermute(head, 'tp', swap)]
  transfers between devices with their start and end apart: 2 -> 1, of which waited for: 1 -> 0; matrix products, arithmetic and copies ran while one was open for 4% -> 3% of each run, Pallas kernels for 22% -> 21%
where the time goes in v3:
time: 79.3 us; the launch traced here: 78.7 us
  Pallas kernels  66.1 us (83%)
  local copies, waits for them, and re-layouts  5.66 us (7%)
  starting transfers between devices  3.03 us (4%)
  other arithmetic  2.52 us (3%)
  between operations  1.33 us (2%)
    pallas_call x1, Pallas kernels, fused(): pl.pallas_call(functools.partial(fused_kernel, n_req, heads, 128 ** (-0.5...  49.2 us
    pallas_call x1, Pallas kernels, prep(): pl.pallas_call(functools.partial(prep_kernel, groups, tokens), grid=(step...  16.9 us
    unnamed x6, local copies, waits for them, and re-layouts  4.47 us
    ppermute x1, starting transfers between devices, local(): head = lax.ppermute(head, 'tp', swap)  3.03 us
    mul x2, other arithmetic, places_tables(): jnp.sin(angles) * jnp.where(lane < 64, -1.0, 1.0)[None, :]  2.51 us
  transfers between devices with their start and end apart: 1, of which 0 were waited for; matrix products, arithmetic and copies ran while one was open for 3% of the time, Pallas kernels for 21%

profile of v3, /device:TPU:0, one launch (start us, length us, event | category | flops | bytes accessed | tf_op | source)
XLA Modules:
  0.0 78.7 jit_solution(6258340659040849116)
XLA Ops:
  0.6 1.2 %slice.3 = bf16[384,1024]{1,0:T(8,128)(2,1)S(1)} slice(bf16[512,1024]{1,0:T(8,128)(2,1)} %own_pre.1), slice={[0:384], [0:1024]} | slice | bytes 1572864 | tf_op jit(solution)/shard_map/slice | solution.py:655
  1.8 3.0 %collective-permute-start = (bf16[384,1024]{1,0:T(8,128)(2,1)S(1)}, bf16[384,1024]{1,0:T(8,128)(2,1)S(1)}, u32[]{:S(2)}, u32[]{:S(2)}) collective-permute-start(bf16[384,1024]{1,0:T(8,128)(2,1)S(1)} %slice.3), channel_id=1, source_target_pairs={{0,1},{1,0},{2,3},{3,2},{4,5},{5,4},{6,7},{7,6},{8,9},{9,8},{10,11... | collective-permute-start | bytes 2359304 | tf_op jit(solution)/shard_map/ppermute | solution.py:656
  5.5 0.0 copy-start.1
  5.5 16.9 %prep.1 = (bf16[2048,1536]{1,0:T(8,128)(2,1)}, bf16[2048,1024]{1,0:T(8,128)(2,1)}, bf16[2048,1024]{1,0:T(8,128)(2,1)}) custom-call(bf16[24576,128]{1,0:T(8,128)(2,1)} %bitcast.8, bf16[16384,128]{1,0:T(8,128)(2,1)} %bitcast.9, bf16[16384,128]{1,0:T(8,128)(2,1)} %bitcast.10), custom_call_target="tpu_custom_call" | custom-call | flops 2000000000 | bytes 29360128 | tf_op jit(solution)/shard_map/prep/pallas_call | solution.py:55
  22.4 0.0 copy-done.1
  22.4 0.7 fusion.1
  23.2 1.8 %fusion = (f32[512,128]{1,0:T(8,128)}, f32[512,128]{1,0:T(8,128)}) fusion(f32[128]{0:T(128)S(1)} %get-tuple-element.12, f32[128]{0:T(128)S(1)} %get-tuple-element.13, f32[512]{0:T(512)S(1)} %add_convert_fusion), kind=kLoop, calls=%fused_computation.2 | loop fusion | flops 131072 | bytes 527360 | tf_op jit(solution)/shard_map/mul | solution.py:555
  24.9 0.0 collective-permute-done.peer_pre
  25.0 0.0 copy-start
  25.0 0.9 %copy-done = bf16[384,1024]{1,0:T(8,128)(2,1)} copy-done((bf16[384,1024]{1,0:T(8,128)(2,1)}, bf16[384,1024]{1,0:T(8,128)(2,1)S(1)}, u32[]{:S(2)}) %copy-start) | copy-done | bytes 786456
  25.8 49.2 %fused.1 = (bf16[8,1024]{1,0:T(8,128)(2,1)}, bf16[512,1024]{1,0:T(8,128)(2,1)}) custom-call(bf16[8,1024]{1,0:T(8,128)(2,1)} %own_dec.1, bf16[512,1024]{1,0:T(8,128)(2,1)} %own_pre.1, bf16[384,1024]{1,0:T(8,128)(2,1)} %copy-done, bf16[2048,1536]{1,0:T(8,128)(2,1)} %get-tuple-element.5.w_hbm, bf16[2048,1024]{1,0:T(8,128)(2,1)} %get-tuple-element.6.prefix_hbm, ...), custom_call_target="tpu_custom_call" | custom-call | tf_op jit(solution)/shard_map/fused/pallas_call | solution.py:572
  75.1 1.3 %copy.16 = bf16[8,1024]{1,0:T(8,128)(2,1)} copy(bf16[8,1024]{1,0:T(8,128)(2,1)} %get-tuple-element.16) | data formatting | bytes 32768
  76.4 2.3 %copy.17 = bf16[512,1024]{1,0:T(8,128)(2,1)} copy(bf16[512,1024]{1,0:T(8,128)(2,1)} %get-tuple-element.17) | data formatting | bytes 2097152
  (3 shorter events, 0.0 us)
Async XLA Ops:
  1.8 23.1 %collective-permute-start = (bf16[384,1024]{1,0:T(8,128)(2,1)S(1)}, bf16[384,1024]{1,0:T(8,128)(2,1)S(1)}, u32[]{:S(2)}, u32[]{:S(2)}) collective-permute-start(bf16[384,1024]{1,0:T(8,128)(2,1)S(1)} %slice.3), channel_id=1, source_target_pairs={{0,1},{1,0},{2,3},{3,2},{4,5},{5,4},{6,7},{7,6},{8,9},{9,8},{10,11... | collective-permute-start | bytes 2359304 | tf_op jit(solution)/shard_map/ppermute | solution.py:656
  5.5 16.9 %copy-start.1 = (s32[8]{0:T(128)S(1)}, s32[8]{0:T(128)}, u32[]{:S(2)}) copy-start(s32[8]{0:T(128)} %lens.1) | copy-start | bytes 100
  25.0 0.9 %copy-start = (bf16[384,1024]{1,0:T(8,128)(2,1)}, bf16[384,1024]{1,0:T(8,128)(2,1)S(1)}, u32[]{:S(2)}) copy-start(bf16[384,1024]{1,0:T(8,128)(2,1)S(1)} %collective-permute-done.peer_pre) | copy-start | bytes 2359300
